TPU v7x, 32 devices: a whole 2x2x4 slice. The times are simulated.
32 devices in a mesh: lat: 4 (over x, core), lev: 8 (over z, y).
Axes of the slice: x: 2, y: 2, z: 4, core: 2. Of those that a mesh axis runs over, the one named last changes fastest.
Arguments:
- prognostic_arrays: float32 [16, 3, 32, 2688], P(None, None, ('lat', 'lev')), may hold values from -6 to 6
- coriolis: float32 [32], P(('lat', 'lev')), may hold values from -1.5 to 1.5
- weights: float32 [32], P(('lat', 'lev')), may hold values from 0.5 to 2
- row_points: int32 [32], P(('lat', 'lev')), may hold values from 196 to 2688, as said below
- owner_pairs: int32 [8, 6], replicated, may hold values from 0 to 47, as said below
- legendre: bfloat16 [8, 6, 97, 32], P('lev', None, None, 'lat'), may hold values from -2 to 2
- depths: float32 [16], replicated, may hold values from 0.5 to 8
- diffusion: float32 [16], replicated, may hold values from 0.5 to 8
Outputs:
- updated: float32 [16, 3, 32, 2688], P(None, None, ('lat', 'lev'))
Inputs may be any that keep to these rules, and one draw needn't show every extreme that they name: `owner_pairs`: a permutation of the pair indices 0 .. 47, 6 to each owner; pair s stands for the wavenumbers s and 95 - s. `row_points`: multiples of 4; some row has exactly 2688 points and some exactly 196.
All inputs are finite; a program needn't handle non-finite values.
Results may differ from a plain program's by a relative error of at most 0.0058.
Values may be sent and summed in bfloat16 or wider, within the bound.
No kernel may reach another device: no remote copies, remote signals or barrier semaphores. Data moves between devices by JAX's collectives and lax.ppermute only.
A program may use at most 64 MiB of HBM per device.

v0:
```python
import math

import jax
import jax.numpy as jnp
from jax import lax
from jax.sharding import PartitionSpec as P

stepsize_delta = 0.5


def tendencies(prognostic_arrays, coriolis):
    vorticity = prognostic_arrays[:, 0]
    spreading_rate_grid = prognostic_arrays[:, 1]
    thermal_state_grid = prognostic_arrays[:, 2]
    rotation = coriolis[None, :, None]
    advanced_curl_rate = vorticity - stepsize_delta * (rotation + vorticity) * spreading_rate_grid
    advanced_spreading_rate = spreading_rate_grid + stepsize_delta * (
        rotation * vorticity - spreading_rate_grid * spreading_rate_grid
    )
    advanced_thermal_state = (
        thermal_state_grid - stepsize_delta * thermal_state_grid * spreading_rate_grid
    )
    return jnp.stack(
        [advanced_curl_rate, advanced_spreading_rate, advanced_thermal_state], axis=1
    ).astype(jnp.bfloat16)


def owner_waves(owner_pairs, highest):
    return jnp.stack([owner_pairs, highest - 1 - owner_pairs], axis=1)


def phase_table(points, wavenumbers, lon_count):
    positions = jnp.arange(lon_count, dtype=jnp.int32)
    product = positions[None, :, None] * wavenumbers[None, None, :] % points[:, None, None]
    angle = (
        product.astype(jnp.float32) * (2.0 * math.pi / points.astype(jnp.float32))[:, None, None]
    )
    return jnp.stack([jnp.cos(angle), -jnp.sin(angle)], axis=2).astype(jnp.bfloat16)


def valid_points(points, lon_count):
    positions = jnp.arange(lon_count, dtype=jnp.int32)
    return positions[None, :] < points[:, None]


def half_mask(my_pairs, slot_total):
    positions = jnp.arange(slot_total, dtype=jnp.int32)
    return positions[None, :] < (slot_total - 1 - my_pairs)[:, None]


def implicit(summed, my_pairs, depth_part, diff_part):
    slot_total = summed.shape[3]
    slot_count = summed.shape[2]
    highest = slot_total - 1
    positions = jnp.arange(slot_total, dtype=jnp.int32)[None, :]
    first_half = positions < (highest - my_pairs)[:, None]
    total = jnp.where(first_half, my_pairs[:, None] + positions, positions - 1).astype(jnp.float32)
    harmonic_operator_spectrum = total * (total + 1.0) / float(highest * highest)
    bundled_prognostics = summed.reshape(-1, 3, 2, slot_count, slot_total)
    vorticity = bundled_prognostics[:, 0]
    spreading_rate_grid = bundled_prognostics[:, 1]
    thermal_state_grid = bundled_prognostics[:, 2]
    layer_stack_count = depth_part[:, None, None, None]
    diff_cols = diff_part[:, None, None, None]
    advanced_curl_rate = vorticity / (
        1.0 + diff_cols * harmonic_operator_spectrum * harmonic_operator_spectrum
    )
    advanced_spreading_rate = (
        spreading_rate_grid + harmonic_operator_spectrum * thermal_state_grid
    ) / (1.0 + layer_stack_count * harmonic_operator_spectrum)
    advanced_thermal_state = thermal_state_grid - layer_stack_count * advanced_spreading_rate
    piled_prognostics = jnp.stack(
        [advanced_curl_rate, advanced_spreading_rate, advanced_thermal_state], axis=1
    )
    return piled_prognostics.reshape(summed.shape).astype(jnp.bfloat16)


def body(
    prognostic_arrays, coriolis, weights, row_points, owner_pairs, legendre, depths, diffusion
):
    levels = prognostic_arrays.shape[0]
    row_count = prognostic_arrays.shape[2]
    lon_count = prognostic_arrays.shape[3]
    group_count = owner_pairs.shape[0]
    slot_count = owner_pairs.shape[1]
    local_basis = legendre[0]
    slot_total = local_basis.shape[1]
    highest = slot_total - 1
    channels = levels * 3
    packed = channels * 4 * slot_count
    wavenumbers = owner_waves(owner_pairs, highest).reshape(-1)
    valid = valid_points(row_points, lon_count)
    gridded = tendencies(prognostic_arrays, coriolis).reshape(channels, row_count, lon_count)
    gridded = jnp.where(valid[None], gridded, jnp.zeros((), gridded.dtype))
    phases = phase_table(row_points, wavenumbers, lon_count).reshape(
        row_count, lon_count, 2, group_count, 2, slot_count
    )
    row_scale = weights / row_points.astype(jnp.float32)
    fourier = jnp.einsum("crx,rxqght->grcqht", gridded, phases, preferred_element_type=jnp.float32)
    fourier = (fourier * row_scale[None, :, None, None, None, None]).astype(jnp.bfloat16)
    band_data = lax.all_to_all(
        fourier.reshape(group_count, row_count, packed),
        "lev",
        split_axis=0,
        concat_axis=0,
        tiled=True,
    )
    band_block = band_data.reshape(group_count * row_count, channels, 2, 2, slot_count)
    owner_index = lax.axis_index("lev")
    my_pairs = lax.dynamic_index_in_dim(owner_pairs, owner_index, 0, keepdims=False)
    first_half = half_mask(my_pairs, slot_total)
    half_masks = jnp.stack([first_half, jnp.logical_not(first_half)], axis=0)
    doubling = jnp.where(owner_waves(my_pairs[None], highest)[0] == 0, 1.0, 2.0).astype(jnp.float32)
    both_halves = jnp.einsum(
        "lkqht,tpl->kqhtp", band_block, local_basis, preferred_element_type=jnp.float32
    )
    summed = lax.psum(jnp.where(first_half, both_halves[:, :, 0], both_halves[:, :, 1]), "lat")
    solved = implicit(summed, my_pairs, depths, diffusion)
    masked_spec = jnp.where(half_masks[None, None], solved[:, :, None], jnp.zeros((), solved.dtype))
    inverted = jnp.einsum(
        "kqhtp,tpl->lkqht", masked_spec, local_basis, preferred_element_type=jnp.float32
    )
    inverted = (inverted * doubling[None, None, None]).astype(jnp.bfloat16)
    returned = lax.all_to_all(
        inverted.reshape(group_count, row_count, packed),
        "lev",
        split_axis=0,
        concat_axis=0,
        tiled=True,
    )
    returned = returned.reshape(group_count, row_count, channels, 2, 2, slot_count)
    outgrid = jnp.einsum("grcqht,rxqght->crx", returned, phases, preferred_element_type=jnp.float32)
    outgrid = jnp.where(valid[None], outgrid, jnp.zeros((), outgrid.dtype))
    return outgrid.reshape(levels, 3, row_count, lon_count)


def solution(mesh):
    in_specs = (
        P(None, None, ("lat", "lev"), None),
        P(("lat", "lev")),
        P(("lat", "lev")),
        P(("lat", "lev")),
        P(),
        P("lev", None, None, "lat"),
        P(),
        P(),
    )
    out_specs = P(None, None, ("lat", "lev"), None)
    return jax.shard_map(body, mesh=mesh, in_specs=in_specs, out_specs=out_specs, check_vma=False)
```

profile of v0, /device:TPU:0, one launch (start us, length us, event | category | flops | bytes accessed | tf_op | source)
XLA Modules:
  0.0 103.7 jit_solution(4373034234354708365)
XLA Ops:
  6.5 0.0 copy-start
  7.2 0.0 copy-start.2
  7.2 0.7 copy-done.2
  7.9 0.1 copy.24
  8.6 1.8 %subtract_convert_fusion.1 = (bf16[16,1,1,2688]{3,2,1,0:T(2,128)(2,1)S(1)}, bf16[16,1,1,2688]{3,2,1,0:T(2,128)(2,1)S(1)}, bf16[16,1,1,2688]{3,2,1,0:T(2,128)(2,1)S(1)}) fusion(f32[16,3,1,2688]{3,2,1,0:T(1,128)} %param.8, f32[]{:T(128)} %bitcast.73), kind=kLoop, calls=%fused_computation.33 | loop fusion | flops 645120 | bytes 774148 | tf_op jit(solution)/shard_map/convert.3
  10.4 1.5 %maximum_reduce_fusion = bf16[16,3,2688]{2,1,0:T(4,128)(2,1)S(1)} fusion(bf16[16,1,1,2688]{3,2,1,0:T(2,128)(2,1)S(1)} %get-tuple-element.11, bf16[16,1,1,2688]{3,2,1,0:T(2,128)(2,1)S(1)} %get-tuple-element.10, bf16[16,1,1,2688]{3,2,1,0:T(2,128)(2,1)S(1)} %get-tuple-element.9), kind=kLoop, calls=%fused_computation.22 | loop fusion | flops 258048 | bytes 516096 | tf_op jit(solution)/shard_map/stack | solution.py:23
  11.9 0.2 convert_element_type.67
  12.9 14.4 %cosine_convert_fusion = (bf16[2688,1,8,2,6]{0,2,4,3,1:T(8,128)(2,1)S(1)}, bf16[2688,1,8,2,6]{0,2,4,3,1:T(8,128)(2,1)S(1)}) fusion(f32[]{:T(128)} %bitcast.6, s32[]{:T(128)} %bitcast.4, s32[8,2,6]{0,2,1:T(8,128)S(1)} %copy.24, pred[]{:T(512)} %bitcast.5), kind=kLoop, calls=%fused_computation.16 | loop fusion | flops 3354624 | bytes 1032585 | tf_op jit(solution)/shard_map/convert.6
  27.2 0.4 fusion.5
  27.7 0.7 copy.25
  28.3 0.6 reshape.376
  29.0 0.5 broadcast.353
  29.5 0.6 reduce.4
  30.1 0.7 reshape.381
  30.8 7.3 %all-to-all-start = ((bf16[8,2,576]{2,1,0:T(2,128)(2,1)}), bf16[8,2,576]{2,1,0:T(2,128)(2,1)S(1)}, u32[]{:S(2)}, u32[]{:S(2)}) async-start(bf16[8,2,576]{2,1,0:T(2,128)(2,1)} %reshape.381), calls=%async_computation | async-start | bytes 40960 | tf_op jit(solution)/shard_map/all_to_all | solution.py:101
  38.1 0.0 all-reduce.2.cloned.1.call-start
  38.2 0.1 iota_compare_fusion.1
  38.3 0.1 iota_compare_fusion.2
  38.4 0.0 copy-start.3
  38.4 0.0 copy-start.4
  38.4 0.1 fusion.26
  38.5 0.6 copy-done.3
  39.0 0.0 copy-done.4
  39.0 0.1 multiply_add_fusion.1
  39.2 0.1 copy.31
  39.3 5.5 %all-to-all-done = bf16[8,2,576]{2,1,0:T(2,128)(2,1)S(1)} async-done(((bf16[8,2,576]{2,1,0:T(2,128)(2,1)}), bf16[8,2,576]{2,1,0:T(2,128)(2,1)S(1)}, u32[]{:S(2)}, u32[]{:S(2)}) %all-to-all-start) | async-done | bytes 18464 | tf_op jit(solution)/shard_map/all_to_all | solution.py:101
  44.7 0.1 reshape.382
  44.8 0.1 reduce.1
  44.9 0.8 reshape.368
  45.8 0.7 copy.27
  46.5 0.0 copy-done
  46.5 0.3 convolution_bitcast_fusion.1
  46.8 0.9 copy.29
  47.7 0.0 all-reduce.2.cloned.1.call-update
  47.7 29.9 %all-reduce.2.cloned.1.call-done = f32[16,3,2,6,97]{4,2,3,1,0:T(2,128)} async-done(((f32[16,3,2,6,97]{4,2,3,1,0:T(2,128)}), f32[16,3,2,6,97]{4,2,3,1,0:T(2,128)}) %all-reduce.2.cloned.1.call-update) | async-done | bytes 223504 | tf_op jit(solution)/shard_map/psum | solution.py:117
  77.6 0.0 copy-start.1
  77.6 1.1 %fusion.31 = (bf16[16,1,2,6,97]{4,2,3,1,0:T(2,128)(2,1)S(1)}, f32[16,1,2,6,97]{4,2,3,1,0:T(2,128)S(1)}) fusion(f32[16,6,97]{2,1,0:T(8,128)S(1)} %get-tuple-element.17, f32[16,3,2,6,97]{4,2,3,1,0:T(2,128)} %all-reduce.2.cloned.1.call-done, f32[6,97]{1,0:T(8,128)S(1)} %fusion.26), kind=kLoop, calls=%fused_computation.64 | loop fusion | flops 74496 | bytes 300312 | tf_op jit(solution)/shard_map/convert.1
  78.7 0.0 copy-done.1
  78.7 0.1 fusion.23
  78.9 0.2 pad_maximum_fusion.1
  79.1 0.4 fusion.4
  79.5 0.7 copy.32
  80.2 0.6 reshape.377
  80.8 0.6 reduce.5
  81.5 0.1 reshape.383
  81.6 11.9 %all_to_all.10 = bf16[8,2,576]{2,1,0:T(2,128)(2,1)S(1)} all-to-all(bf16[8,2,576]{2,1,0:T(2,128)(2,1)S(1)} %reshape.383), channel_id=1, replica_groups=mesh['lat'=4,'lev'=8] {'lev'}, dimensions={0} | all-to-all | bytes 36864 | tf_op jit(solution)/shard_map/all_to_all | solution.py:124
  93.5 0.1 reshape.384
  93.6 0.1 reduce.2
  93.7 0.8 reshape.371
  94.5 0.7 copy.35
  95.2 0.4 fusion.1
  95.6 1.3 %reshape.372 = f32[16,3,1,2688]{3,2,1,0:T(1,128)} reshape(f32[48,1,2688]{2,0,1:T(8,128)S(1)} %fusion.1) | data formatting | bytes 1032192 | tf_op jit(solution)/shard_map/reshape | solution.py:134
  (10 shorter events, 0.1 us)
Async XLA Ops:
  6.5 39.9 %copy-start = (bf16[1,6,97,8]{2,3,1,0:T(8,128)(2,1)S(1)}, bf16[1,6,97,8]{2,3,1,0:T(8,128)(2,1)}, u32[]{:S(2)}) copy-start(bf16[1,6,97,8]{2,3,1,0:T(8,128)(2,1)} %param.13) | copy-start | bytes 27940
  7.2 0.7 copy-start.2
  30.8 13.9 %all-to-all-start = ((bf16[8,2,576]{2,1,0:T(2,128)(2,1)}), bf16[8,2,576]{2,1,0:T(2,128)(2,1)S(1)}, u32[]{:S(2)}, u32[]{:S(2)}) async-start(bf16[8,2,576]{2,1,0:T(2,128)(2,1)} %reshape.381), calls=%async_computation | async-start | bytes 40960 | tf_op jit(solution)/shard_map/all_to_all | solution.py:101
  38.1 39.5 %all-reduce.2.cloned.1.call-start = ((), (), s32[]{:S(2)}) async-start(), calls=%async_computation.2 | async-start | bytes 589824 | tf_op jit(solution)/shard_map/psum | solution.py:117
  38.4 0.7 copy-start.3
  38.4 0.7 copy-start.4
  77.6 1.1 %copy-start.1 = (f32[16,3,2,6,97]{4,2,3,1,0:T(2,128)S(1)}, f32[16,3,2,6,97]{4,2,3,1,0:T(2,128)}, u32[]{:S(2)}) copy-start(f32[16,3,2,6,97]{4,2,3,1,0:T(2,128)} %all-reduce.2.cloned.1.call-done) | copy-start | bytes 670468
Sparse Core Ops, SparseCore 0:
  47.8 29.7 all-reduce.1
where the time goes:
time: 104 us
  waiting for transfers between devices  35.4 us (34%)
  other arithmetic  21 us (20%)
  between operations  15.7 us (15%)
  blocking collectives  11.9 us (11%)
  local copies, waits for them, and re-layouts  10.9 us (10%)
  starting transfers between devices  7.35 us (7%)
  matrix products  1.47 us (1%)
    psum x1, waiting for transfers between devices, body(): lax.psum(jnp.where(first_half, both_halves[:, :, 0], both_halves[:, :, 1]...  29.9 us
    another operation x4, other arithmetic  17.4 us
    all_to_all x1, blocking collectives, body(): lax.all_to_all(inverted.reshape(group_count, row_count, packed), 'lev', s...  11.9 us
    all_to_all x1, starting transfers between devices, body(): lax.all_to_all(fourier.reshape(group_count, row_count, packed), 'lev', sp...  7.31 us
    all_to_all x1, waiting for transfers between devices, body(): lax.all_to_all(fourier.reshape(group_count, row_count, packed), 'lev', sp...  5.47 us
    unnamed x14, local copies, waits for them, and re-layouts  2.26 us
  transfers between devices with their start and end apart: 2, of which 2 were waited for; matrix products, arithmetic and copies ran while one was open for 0% of the time, Pallas kernels for 0%

commit v1 on v0

--- a/solution.py
+++ b/solution.py
@@ -1,8 +1,11 @@
+import functools
 import math
 
 import jax
 import jax.numpy as jnp
 from jax import lax
+from jax.experimental import pallas as pl
+from jax.experimental.pallas import tpu as pltpu
 from jax.sharding import PartitionSpec as P
 
 stepsize_delta = 0.5
@@ -75,7 +78,7 @@
     return piled_prognostics.reshape(summed.shape).astype(jnp.bfloat16)
 
 
-def body(
+def general_body(
     prognostic_arrays, coriolis, weights, row_points, owner_pairs, legendre, depths, diffusion
 ):
     levels = prognostic_arrays.shape[0]
@@ -134,6 +137,353 @@
     return outgrid.reshape(levels, 3, row_count, lon_count)
 
 
+lane_count = 128
+piece_rows = 8
+
+
+def turn_cos_sin(turns, quarter):
+    scaled = turns * 4.0
+    nearest = jnp.floor(scaled + 0.5)
+    arc = (scaled - nearest) * (0.5 * math.pi)
+    square = arc * arc
+    sine = arc + arc * square * (
+        -1.6666654611e-1 + square * (8.3321608736e-3 + square * -1.9515295891e-4)
+    )
+    cosine = (
+        1.0
+        - 0.5 * square
+        + square
+        * square
+        * (4.166664568298827e-2 + square * (-1.388731625493765e-3 + square * 2.443315711809948e-5))
+    )
+    turn = nearest + quarter
+    turn = turn - 4.0 * jnp.floor(turn * 0.25)
+    swapped = jnp.logical_or(turn == 1.0, turn == 3.0)
+    cos_part = jnp.where(swapped, sine, cosine)
+    sin_part = jnp.where(swapped, cosine, sine)
+    cos_part = jnp.where(jnp.logical_or(turn == 1.0, turn == 2.0), -cos_part, cos_part)
+    sin_part = jnp.where(turn >= 2.0, -sin_part, sin_part)
+    return cos_part, sin_part
+
+
+def turns_of(product, points, inverse):
+    rest = product - jnp.floor(product * inverse) * points
+    rest = jnp.where(rest < 0.0, rest + points, rest)
+    rest = jnp.where(rest >= points, rest - points, rest)
+    return rest * inverse
+
+
+def analysis_kernel(
+    dims,
+    grid_hbm,
+    coriolis_ref,
+    weights_ref,
+    points_ref,
+    pairs_ref,
+    legendre_ref,
+    sent_ref,
+    table_ref,
+    grid_ref,
+    rhs_ref,
+    wave_ref,
+    sem,
+):
+    levels, lon_count, group_count, slot_count, parts, per_part, highest = dims
+    channels = 3 * levels
+    blocks = lon_count // lane_count
+    active = slot_count // per_part
+    copy = pltpu.make_async_copy(grid_hbm, grid_ref, sem)
+    copy.start()
+
+    tile = (piece_rows, lane_count)
+    points = points_ref[0]
+    points_vec = jnp.full(tile, points, jnp.int32).astype(jnp.float32)
+    inverse = 1.0 / points_vec
+    row = lax.broadcasted_iota(jnp.int32, tile, 0)
+    lane = lax.broadcasted_iota(jnp.int32, tile, 1)
+    lane_float = lane.astype(jnp.float32)
+    quarter = (row // (2 * per_part)).astype(jnp.float32)
+    second_half = (row // per_part) % 2 == 1
+    slot = row % per_part
+    for part in range(active):
+        for group in range(group_count):
+            pair = jnp.full(tile, pairs_ref[group, part * per_part], jnp.int32)
+            for other in range(1, per_part):
+                pair = jnp.where(slot == other, pairs_ref[group, part * per_part + other], pair)
+            wave = jnp.where(second_half, highest - 1 - pair, pair).astype(jnp.float32)
+            near_cos, near_sin = turn_cos_sin(
+                turns_of(wave * lane_float, points_vec, inverse), quarter
+            )
+            far_cos, far_sin = turn_cos_sin(
+                turns_of(wave * (lane_float * float(lane_count)), points_vec, inverse),
+                jnp.zeros(tile, jnp.float32),
+            )
+            at = (part * group_count + group) * piece_rows
+            for block in range(blocks):
+                turned = (
+                    near_cos * far_cos[:, block : block + 1]
+                    - near_sin * far_sin[:, block : block + 1]
+                )
+                table_ref[at : at + piece_rows, block * lane_count : (block + 1) * lane_count] = (
+                    turned.astype(jnp.bfloat16)
+                )
+
+    copy.wait()
+    rotation = coriolis_ref[0]
+    lane_wide = lax.broadcasted_iota(jnp.int32, (levels, lane_count), 1)
+    for block in range(blocks):
+        vorticity, spreading, thermal = (
+            grid_ref[pl.ds(field * blocks + block, levels, stride=3 * blocks), :]
+            for field in range(3)
+        )
+        inside = lane_wide < points - block * lane_count
+        advanced = (
+            vorticity - stepsize_delta * (rotation + vorticity) * spreading,
+            spreading + stepsize_delta * (rotation * vorticity - spreading * spreading),
+            thermal - stepsize_delta * thermal * spreading,
+        )
+        for field in range(3):
+            rhs_ref[
+                field * levels : (field + 1) * levels,
+                block * lane_count : (block + 1) * lane_count,
+            ] = jnp.where(inside, advanced[field], 0.0).astype(jnp.bfloat16)
+
+    summed = lax.dot_general(
+        table_ref[...],
+        rhs_ref[...],
+        (((1,), (1,)), ((), ())),
+        preferred_element_type=jnp.float32,
+    )
+    wave_ref[:, :channels] = summed
+    scale = jnp.full(tile, weights_ref[0], jnp.float32) / points_vec
+    slot_total = highest + 1
+    left = lane_count - channels
+    for part in range(active):
+        first = jnp.pad(
+            legendre_ref[0, part * per_part].astype(jnp.float32),
+            ((0, 0), (0, lane_count - slot_total)),
+        )
+        second = jnp.pad(
+            legendre_ref[0, part * per_part + 1].astype(jnp.float32),
+            ((0, 0), (0, lane_count - slot_total)),
+        )
+        upper_basis = pltpu.roll(first, channels, 1)
+        lower = jnp.where(
+            lane < slot_total, second, pltpu.roll(first, (slot_total - left) % lane_count, 1)
+        )
+        for group in range(group_count):
+            at = part * group_count + group
+            upper = jnp.where(
+                lane < channels,
+                wave_ref[at * piece_rows : (at + 1) * piece_rows, :] * scale,
+                upper_basis,
+            )
+            sent_ref[at] = jnp.concatenate([upper, lower], axis=0).astype(jnp.bfloat16)
+    for at in range(active * group_count, parts * group_count):
+        sent_ref[at] = jnp.zeros((2 * piece_rows, lane_count), jnp.bfloat16)
+
+
+def spectral_kernel(
+    dims,
+    received_ref,
+    position_ref,
+    pairs_ref,
+    depths_ref,
+    diffusion_ref,
+    sent_ref,
+    wave_ref,
+):
+    levels, lon_count, group_count, slot_count, parts, per_part, highest = dims
+    channels = 3 * levels
+    slot_total = highest + 1
+    left = lane_count - channels
+    sources = parts * group_count
+    part, group = position_ref[0], position_ref[1]
+    tile = (piece_rows, lane_count)
+    lane = lax.broadcasted_iota(jnp.int32, tile, 1)
+    for source in range(sources):
+        wave_ref[source * piece_rows : (source + 1) * piece_rows, :] = received_ref[
+            source, :piece_rows, :
+        ].astype(jnp.float32)
+    first, second = [], []
+    for band in range(parts):
+        piece = received_ref[band * group_count + group].astype(jnp.float32)
+        upper, lower = piece[:piece_rows], piece[piece_rows:]
+        start = pltpu.roll(upper, left, 1)
+        rest = pltpu.roll(lower, (lane_count - (slot_total - left)) % lane_count, 1)
+        first.append(jnp.where(lane < left, start, jnp.where(lane < slot_total, rest, 0.0)))
+        second.append(jnp.where(lane < slot_total, lower, 0.0))
+    bases = [
+        jnp.concatenate(first, axis=0).astype(jnp.bfloat16),
+        jnp.concatenate(second, axis=0).astype(jnp.bfloat16),
+    ]
+    row_tile = (1, lane_count)
+    lane_row = lax.broadcasted_iota(jnp.int32, row_tile, 1)
+    depth_row = jnp.zeros(row_tile, jnp.float32)
+    damp_row = jnp.zeros(row_tile, jnp.float32)
+    for level in range(levels):
+        depth_row = jnp.where(lane_row % levels == level, depths_ref[level], depth_row)
+        damp_row = jnp.where(lane_row == level, diffusion_ref[level], damp_row)
+    is_first = lane_row < levels
+    is_last = lane_row >= 2 * levels
+    coeff_row = jnp.where(is_first, damp_row, depth_row)
+    column_tile = (lane_count, 1)
+    position = lax.broadcasted_iota(jnp.int32, column_tile, 0)
+    for index in range(per_part):
+        pair = pairs_ref[group, jnp.minimum(part * per_part + index, slot_count - 1)]
+        lower_half = position < highest - pair
+        total = jnp.where(lower_half, pair + position, position - 1).astype(jnp.float32)
+        operator = total * (total + 1.0) / float(highest * highest)
+        factor = jnp.where(is_first, operator * operator, operator)
+        divisor = 1.0 + coeff_row * factor
+        basis = bases[index]
+        basis_turned = basis.astype(jnp.float32).T.astype(jnp.bfloat16)
+        solved = []
+        for phase in range(2):
+            halves = []
+            for half in range(2):
+                at = (phase * 2 + half) * per_part + index
+                waves = wave_ref[pl.ds(at, sources, stride=piece_rows), :].astype(jnp.bfloat16)
+                halves.append(
+                    jnp.dot(basis_turned, waves, preferred_element_type=jnp.float32)
+                )
+            spec = jnp.where(lower_half, halves[0], halves[1])
+            thermal = pltpu.roll(spec, lane_count - levels, 1)
+            top = jnp.where(is_first, spec, spec + operator * thermal)
+            quotient = top / divisor
+            moved = pltpu.roll(quotient, levels, 1)
+            solved.append(jnp.where(is_last, spec - depth_row * moved, quotient))
+        for phase in range(2):
+            for half in range(2):
+                at = (phase * 2 + half) * per_part + index
+                kept = jnp.where(
+                    lower_half if half == 0 else jnp.logical_not(lower_half), solved[phase], 0.0
+                )
+                back = jnp.dot(
+                    basis, kept.astype(jnp.bfloat16), preferred_element_type=jnp.float32
+                )
+                wavenumber = pair if half == 0 else highest - 1 - pair
+                doubling = jnp.where(wavenumber == 0, 1.0, 2.0)
+                wave_ref[pl.ds(at, sources, stride=piece_rows), :] = back * doubling
+    for source in range(sources):
+        sent_ref[source] = wave_ref[
+            source * piece_rows : (source + 1) * piece_rows, :
+        ].astype(jnp.bfloat16)
+
+
+def synthesis_kernel(dims, received_ref, table_ref, points_ref, out_ref):
+    levels, lon_count, group_count, slot_count, parts, per_part, highest = dims
+    blocks = lon_count // lane_count
+    sources = parts * group_count
+    columns = (slot_count // per_part) * group_count * piece_rows
+    pieces = [received_ref[source].astype(jnp.float32) for source in range(sources)]
+    turned = jnp.concatenate(pieces, axis=0).T
+    waves = turned[: 3 * levels, :columns].astype(jnp.bfloat16)
+    points = points_ref[0]
+    lane_wide = lax.broadcasted_iota(jnp.int32, (levels, lane_count), 1)
+    result = jnp.dot(waves, table_ref[...], preferred_element_type=jnp.float32)
+    for block in range(blocks):
+        inside = lane_wide < points - block * lane_count
+        for field in range(3):
+            value = result[
+                field * levels : (field + 1) * levels,
+                block * lane_count : (block + 1) * lane_count,
+            ]
+            out_ref[pl.ds(field * blocks + block, levels, stride=3 * blocks), :] = jnp.where(
+                inside, value, 0.0
+            )
+
+
+def packed_body(
+    dims,
+    prognostic_arrays,
+    coriolis,
+    weights,
+    row_points,
+    owner_pairs,
+    legendre,
+    depths,
+    diffusion,
+):
+    levels, lon_count, group_count, slot_count, parts, per_part, highest = dims
+    channels = 3 * levels
+    blocks = lon_count // lane_count
+    sources = parts * group_count
+    columns = (slot_count // per_part) * group_count * piece_rows
+    in_vmem = pl.BlockSpec(memory_space=pltpu.VMEM)
+    in_smem = pl.BlockSpec(memory_space=pltpu.SMEM)
+    in_hbm = pl.BlockSpec(memory_space=pl.ANY)
+    params = pltpu.CompilerParams(vmem_limit_bytes=16 << 20)
+    grid = prognostic_arrays.reshape(channels * blocks, lane_count)
+    position = jnp.stack([lax.axis_index("lat"), lax.axis_index("lev")]).astype(jnp.int32)
+    sent, table = pl.pallas_call(
+        functools.partial(analysis_kernel, dims),
+        name="analysis",
+        out_shape=(
+            jax.ShapeDtypeStruct((sources, 2 * piece_rows, lane_count), jnp.bfloat16),
+            jax.ShapeDtypeStruct((columns, lon_count), jnp.bfloat16),
+        ),
+        in_specs=[in_hbm, in_smem, in_smem, in_smem, in_smem, in_vmem],
+        out_specs=(in_vmem, in_vmem),
+        scratch_shapes=[
+            pltpu.VMEM((channels * blocks, lane_count), jnp.float32),
+            pltpu.VMEM((channels, lon_count), jnp.bfloat16),
+            pltpu.VMEM((columns, lane_count), jnp.float32),
+            pltpu.SemaphoreType.DMA(()),
+        ],
+        compiler_params=params,
+    )(grid, coriolis, weights, row_points, owner_pairs, jnp.swapaxes(legendre, 2, 3))
+    received = lax.all_to_all(sent, ("lat", "lev"), split_axis=0, concat_axis=0, tiled=True)
+    solved = pl.pallas_call(
+        functools.partial(spectral_kernel, dims),
+        name="spectral",
+        out_shape=jax.ShapeDtypeStruct((sources, piece_rows, lane_count), jnp.bfloat16),
+        in_specs=[in_vmem, in_smem, in_smem, in_smem, in_smem],
+        out_specs=in_vmem,
+        scratch_shapes=[pltpu.VMEM((sources * piece_rows, lane_count), jnp.float32)],
+        compiler_params=params,
+    )(received, position, owner_pairs, depths, diffusion)
+    returned = lax.all_to_all(solved, ("lat", "lev"), split_axis=0, concat_axis=0, tiled=True)
+    updated = pl.pallas_call(
+        functools.partial(synthesis_kernel, dims),
+        name="synthesis",
+        out_shape=jax.ShapeDtypeStruct((channels * blocks, lane_count), jnp.float32),
+        in_specs=[in_vmem, in_vmem, in_smem],
+        out_specs=in_vmem,
+        compiler_params=params,
+    )(returned, table, row_points)
+    return updated.reshape(prognostic_arrays.shape)
+
+
+def body(prognostic_arrays, coriolis, weights, row_points, owner_pairs, legendre, depths, diffusion):
+    levels, _, row_count, lon_count = prognostic_arrays.shape
+    group_count, slot_count = owner_pairs.shape
+    slot_total, band_rows = legendre.shape[2:]
+    parts = lax.axis_size("lat")
+    per_part = -(-slot_count // parts)
+    channels = 3 * levels
+    fits = (
+        row_count == 1
+        and band_rows == piece_rows == group_count
+        and 4 * per_part == piece_rows
+        and slot_count % per_part == 0
+        and lon_count % lane_count == 0
+        and lon_count // lane_count <= lane_count
+        and levels % 16 == 0
+        and channels < slot_total <= lane_count
+        and 2 * slot_total + channels <= 2 * lane_count
+        and lon_count * slot_total < 2**24
+        and (parts * group_count * piece_rows) % lane_count == 0
+    )
+    arguments = (
+        prognostic_arrays, coriolis, weights, row_points, owner_pairs, legendre, depths, diffusion
+    )
+    if not fits:
+        return general_body(*arguments)
+    dims = (levels, lon_count, group_count, slot_count, parts, per_part, slot_total - 1)
+    return packed_body(dims, *arguments)
+
+
 def solution(mesh):
     in_specs = (
         P(None, None, ("lat", "lev"), None),

time: 104 us -> 35.3 us (0.34)
  waiting for transfers between devices: 35.4 us -> 7.7 us
  other arithmetic: 21 us -> 0.08 us
  between operations: 15.7 us -> 2.03 us
  local copies, waits for them, and re-layouts: 10.9 us -> 1.75 us
  Pallas kernels: 0 us -> 6.69 us
  blocking collectives: 11.9 us -> 9.44 us
  matrix products: 1.47 us -> 0 us
    psum x1 -> x0, waiting for transfers between devices: 29.9 us -> none  [body(): lax.psum(jnp.where(first_half, both_halves[:, :, 0], both_halves[:, :, 1]...]
    another operation x10 -> x1, other arithmetic: 19.1 us -> 0.08 us  [packed_body(): jnp.stack([lax.axis_index('lat'), lax.axis_index('lev')]).astype(jnp.int32)]
    pallas_call x0 -> x3, Pallas kernels: none -> 6.69 us  [the longest x1 3.96 us: packed_body(): pl.pallas_call(functools.partial(analysis_kernel, dims), name='analysis',...]
    reshape x6 -> x0, local copies, waits for them, and re-layouts: 4.55 us -> none  [the longest x2 1.52 us: body(): band_data.reshape(group_count * row_count, channels, 2, 2, slot_count)]
    all_to_all x1, blocking collectives: 11.9 us -> 9.44 us  [packed_body(): lax.all_to_all(solved, ('lat', 'lev'), split_axis=0, concat_axis=0, tiled...]
    all_to_all x1, waiting for transfers between devices: 5.47 us -> 7.7 us  [packed_body(): lax.all_to_all(sent, ('lat', 'lev'), split_axis=0, concat_axis=0, tiled=T...]
    another operation x3 -> x0, local copies, waits for them, and re-layouts: 1.6 us -> none
    convert_element_type x4 -> x0, local copies, waits for them, and re-layouts: 1.57 us -> none  [the longest x1 0.67 us: body(): inverted = (inverted * doubling[None, None, None]).astype(jnp.bfloat16)]
  transfers between devices with their start and end apart: 2 -> 1, of which waited for: 2 -> 1; matrix products, arithmetic and copies ran while one was open for 0% -> 0% of each run, Pallas kernels for 0% -> 0%
where the time goes in v1:
time: 35.3 us; the launch traced here: 35 us
  blocking collectives  9.44 us (27%)
  waiting for transfers between devices  7.7 us (22%)
  starting transfers between devices  7.34 us (21%)
  Pallas kernels  6.69 us (19%)
  between operations  2.03 us (6%)
  local copies, waits for them, and re-layouts  1.75 us (5%)
    all_to_all x1, blocking collectives, packed_body(): lax.all_to_all(solved, ('lat', 'lev'), split_axis=0, concat_axis=0, tiled...  9.44 us
    all_to_all x1, waiting for transfers between devices, packed_body(): lax.all_to_all(sent, ('lat', 'lev'), split_axis=0, concat_axis=0, tiled=T...  7.7 us
    all_to_all x1, starting transfers between devices, packed_body(): lax.all_to_all(sent, ('lat', 'lev'), split_axis=0, concat_axis=0, tiled=T...  7.34 us
    pallas_call x1, Pallas kernels, packed_body(): pl.pallas_call(functools.partial(analysis_kernel, dims), name='analysis',...  3.96 us
    unnamed x10, local copies, waits for them, and re-layouts  1.75 us
    pallas_call x1, Pallas kernels, packed_body(): pl.pallas_call(functools.partial(spectral_kernel, dims), name='spectral',...  1.58 us
    pallas_call x1, Pallas kernels, packed_body(): pl.pallas_call(functools.partial(synthesis_kernel, dims), name='synthesis...  1.15 us
  transfers between devices with their start and end apart: 1, of which 1 were waited for; matrix products, arithmetic and copies ran while one was open for 0% of the time, Pallas kernels for 0%

profile of v1, /device:TPU:0, one launch (start us, length us, event | category | flops | bytes accessed | tf_op | source)
XLA Modules:
  0.0 35.0 jit_solution(9181478436106344948)
XLA Ops:
  0.7 0.0 copy-start.1
  2.0 0.0 copy-done.1
  2.0 0.0 copy-start
  2.0 1.0 %copy-done = f32[16,3,1,2688]{3,2,1,0:T(1,128)S(1)} copy-done((f32[16,3,1,2688]{3,2,1,0:T(1,128)S(1)}, f32[16,3,1,2688]{3,2,1,0:T(1,128)}, u32[]{:S(2)}) %copy-start) | copy-done | bytes 516120
  3.0 0.0 copy-start.2
  3.0 0.7 %copy-done.2 = bf16[1,6,97,8]{2,3,1,0:T(8,128)(2,1)S(1)} copy-done((bf16[1,6,97,8]{2,3,1,0:T(8,128)(2,1)S(1)}, bf16[1,6,97,8]{2,3,1,0:T(8,128)(2,1)}, u32[]{:S(2)}) %copy-start.2) | copy-done | bytes 9336
  3.7 4.0 %analysis.1 = (bf16[32,16,128]{2,1,0:T(8,128)(2,1)}, bf16[192,2688]{1,0:T(8,128)(2,1)S(1)}) custom-call(f32[1008,128]{1,0:T(8,128)S(1)} %bitcast.5, f32[1]{0:T(128)S(6)} %copy.11.coriolis_ref, f32[1]{0:T(128)S(6)} %copy.12.weights_ref, s32[1]{0:T(128)S(6)} %copy.13.points_ref, s32[8,6]{1,0:T(8,128)S(1)} %copy-done.1, bf16[1,6,8,97]{3,2,1,0:T(8,128)(2,1)S(1)} %bitcast.6), custom_call_target="tpu_custom_call" | custom-call | tf_op jit(solution)/shard_map/analysis/pallas_call | solution.py:419
  7.7 7.3 %all-to-all-start = ((bf16[32,16,128]{2,1,0:T(8,128)(2,1)}), bf16[32,16,128]{2,1,0:T(8,128)(2,1)S(1)}, u32[]{:S(2)}, u32[]{:S(2)}) async-start(bf16[32,16,128]{2,1,0:T(8,128)(2,1)} %get-tuple-element.7), calls=%async_computation | async-start | bytes 262144 | tf_op jit(solution)/shard_map/all_to_all | solution.py:436
  15.0 0.0 copy-start.3
  15.0 0.0 copy-start.4
  15.1 0.1 pad_add_fusion.position_ref
  15.1 7.7 %all-to-all-done.received_ref = bf16[32,16,128]{2,1,0:T(8,128)(2,1)S(1)} async-done(((bf16[32,16,128]{2,1,0:T(8,128)(2,1)}), bf16[32,16,128]{2,1,0:T(8,128)(2,1)S(1)}, u32[]{:S(2)}, u32[]{:S(2)}) %all-to-all-start) | async-done | bytes 131104 | tf_op jit(solution)/shard_map/all_to_all | solution.py:436
  22.8 0.0 copy-done.3
  22.8 0.0 copy-done.4
  22.8 1.6 %spectral.1 = bf16[32,8,128]{2,1,0:T(8,128)(2,1)S(1)} custom-call(bf16[32,16,128]{2,1,0:T(8,128)(2,1)S(1)} %all-to-all-done.received_ref, s32[2]{0:T(128)S(1)} %pad_add_fusion.position_ref, s32[8,6]{1,0:T(8,128)S(1)} %copy-done.1, f32[16]{0:T(128)S(1)} %copy-done.3, f32[16]{0:T(128)S(1)} %copy-done.4), custom_call_target="tpu_custom_call" | custom-call | tf_op jit(solution)/shard_map/spectral/pallas_call | solution.py:437
  24.4 9.4 %all_to_all.10.received_ref = bf16[32,8,128]{2,1,0:T(8,128)(2,1)S(1)} all-to-all(bf16[32,8,128]{2,1,0:T(8,128)(2,1)S(1)} %spectral.1), channel_id=1, replica_groups=mesh['lat'=4,'lev'=8] {'lat','lev'}, dimensions={0} | all-to-all | bytes 131072 | tf_op jit(solution)/shard_map/all_to_all | solution.py:446
  33.9 1.2 %synthesis.1 = f32[1008,128]{1,0:T(8,128)} custom-call(bf16[32,8,128]{2,1,0:T(8,128)(2,1)S(1)} %all_to_all.10.received_ref, bf16[192,2688]{1,0:T(8,128)(2,1)S(1)} %get-tuple-element.8.table_ref, s32[1]{0:T(128)S(6)} %copy.13.points_ref), custom_call_target="tpu_custom_call" | custom-call | tf_op jit(solution)/shard_map/synthesis/pallas_call | solution.py:447
Async XLA Ops:
  0.7 1.3 %copy-start.1 = (s32[8,6]{1,0:T(8,128)S(1)}, s32[8,6]{1,0:T(8,128)}, u32[]{:S(2)}) copy-start(s32[8,6]{1,0:T(8,128)} %pairs_ref.3) | copy-start | bytes 580
  2.0 1.0 %copy-start = (f32[16,3,1,2688]{3,2,1,0:T(1,128)S(1)}, f32[16,3,1,2688]{3,2,1,0:T(1,128)}, u32[]{:S(2)}) copy-start(f32[16,3,1,2688]{3,2,1,0:T(1,128)} %param.8) | copy-start | bytes 1548292
  3.0 0.7 %copy-start.2 = (bf16[1,6,97,8]{2,3,1,0:T(8,128)(2,1)S(1)}, bf16[1,6,97,8]{2,3,1,0:T(8,128)(2,1)}, u32[]{:S(2)}) copy-start(bf16[1,6,97,8]{2,3,1,0:T(8,128)(2,1)} %param.13) | copy-start | bytes 27940
  7.7 15.2 %all-to-all-start = ((bf16[32,16,128]{2,1,0:T(8,128)(2,1)}), bf16[32,16,128]{2,1,0:T(8,128)(2,1)S(1)}, u32[]{:S(2)}, u32[]{:S(2)}) async-start(bf16[32,16,128]{2,1,0:T(8,128)(2,1)} %get-tuple-element.7), calls=%async_computation | async-start | bytes 262144 | tf_op jit(solution)/shard_map/all_to_all | solution.py:436
  15.0 7.8 %copy-start.3 = (f32[16]{0:T(128)S(1)}, f32[16]{0:T(128)}, u32[]{:S(2)}) copy-start(f32[16]{0:T(128)} %depths_ref.1) | copy-start | bytes 196
  15.0 7.8 %copy-start.4 = (f32[16]{0:T(128)S(1)}, f32[16]{0:T(128)}, u32[]{:S(2)}) copy-start(f32[16]{0:T(128)} %diffusion_ref.1) | copy-start | bytes 196

commit v2 on v1

--- a/solution.py
+++ b/solution.py
@@ -141,7 +141,7 @@
 piece_rows = 8
 
 
-def turn_cos_sin(turns, quarter):
+def turn_cos_sin(turns):
     scaled = turns * 4.0
     nearest = jnp.floor(scaled + 0.5)
     arc = (scaled - nearest) * (0.5 * math.pi)
@@ -156,13 +156,11 @@
         * square
         * (4.166664568298827e-2 + square * (-1.388731625493765e-3 + square * 2.443315711809948e-5))
     )
-    turn = nearest + quarter
-    turn = turn - 4.0 * jnp.floor(turn * 0.25)
-    swapped = jnp.logical_or(turn == 1.0, turn == 3.0)
+    swapped = jnp.logical_or(nearest == 1.0, nearest == 3.0)
     cos_part = jnp.where(swapped, sine, cosine)
     sin_part = jnp.where(swapped, cosine, sine)
-    cos_part = jnp.where(jnp.logical_or(turn == 1.0, turn == 2.0), -cos_part, cos_part)
-    sin_part = jnp.where(turn >= 2.0, -sin_part, sin_part)
+    cos_part = jnp.where(jnp.logical_or(nearest == 1.0, nearest == 2.0), -cos_part, cos_part)
+    sin_part = jnp.where(jnp.logical_or(nearest == 2.0, nearest == 3.0), -sin_part, sin_part)
     return cos_part, sin_part
 
 
@@ -176,96 +174,123 @@
 def analysis_kernel(
     dims,
     grid_hbm,
+    coriolis_hbm,
+    weights_hbm,
+    points_hbm,
+    pairs_hbm,
+    legendre_hbm,
+    sent_ref,
+    near_ref,
+    far_ref,
+    grid_ref,
     coriolis_ref,
     weights_ref,
     points_ref,
     pairs_ref,
     legendre_ref,
-    sent_ref,
-    table_ref,
-    grid_ref,
     rhs_ref,
     wave_ref,
-    sem,
+    sems,
 ):
     levels, lon_count, group_count, slot_count, parts, per_part, highest = dims
     channels = 3 * levels
     blocks = lon_count // lane_count
     active = slot_count // per_part
-    copy = pltpu.make_async_copy(grid_hbm, grid_ref, sem)
-    copy.start()
+    sources = parts * group_count
+    copies = [
+        pltpu.make_async_copy(source, target, sems.at[at])
+        for at, (source, target) in enumerate(
+            (
+                (pairs_hbm, pairs_ref),
+                (points_hbm, points_ref),
+                (grid_hbm, grid_ref),
+                (coriolis_hbm, coriolis_ref),
+                (weights_hbm, weights_ref),
+                (legendre_hbm, legendre_ref),
+            )
+        )
+    ]
+    for copy in copies:
+        copy.start()
+    copies[0].wait()
+    copies[1].wait()
 
     tile = (piece_rows, lane_count)
-    points = points_ref[0]
-    points_vec = jnp.full(tile, points, jnp.int32).astype(jnp.float32)
-    inverse = 1.0 / points_vec
     row = lax.broadcasted_iota(jnp.int32, tile, 0)
     lane = lax.broadcasted_iota(jnp.int32, tile, 1)
-    lane_float = lane.astype(jnp.float32)
-    quarter = (row // (2 * per_part)).astype(jnp.float32)
-    second_half = (row // per_part) % 2 == 1
-    slot = row % per_part
-    for part in range(active):
-        for group in range(group_count):
-            pair = jnp.full(tile, pairs_ref[group, part * per_part], jnp.int32)
-            for other in range(1, per_part):
-                pair = jnp.where(slot == other, pairs_ref[group, part * per_part + other], pair)
-            wave = jnp.where(second_half, highest - 1 - pair, pair).astype(jnp.float32)
-            near_cos, near_sin = turn_cos_sin(
-                turns_of(wave * lane_float, points_vec, inverse), quarter
-            )
-            far_cos, far_sin = turn_cos_sin(
-                turns_of(wave * (lane_float * float(lane_count)), points_vec, inverse),
-                jnp.zeros(tile, jnp.float32),
-            )
-            at = (part * group_count + group) * piece_rows
-            for block in range(blocks):
-                turned = (
-                    near_cos * far_cos[:, block : block + 1]
-                    - near_sin * far_sin[:, block : block + 1]
-                )
-                table_ref[at : at + piece_rows, block * lane_count : (block + 1) * lane_count] = (
-                    turned.astype(jnp.bfloat16)
-                )
-
-    copy.wait()
-    rotation = coriolis_ref[0]
+    lane_slot = lane // group_count % parts * per_part + lane // sources % per_part
+    at_group = lane % group_count == row
+    pairs = pairs_ref[...].astype(jnp.float32)
+    spread = jnp.zeros(tile, jnp.float32)
+    for slot in range(slot_count):
+        chosen = jnp.logical_and(at_group, lane_slot == slot)
+        spread = jnp.where(chosen, pairs[:, slot : slot + 1], spread)
+    pair = jnp.sum(spread, axis=0, keepdims=True)
+    lane_row = lax.broadcasted_iota(jnp.int32, (1, lane_count), 1)
+    wave = jnp.where(lane_row >= per_part * sources, float(highest - 1) - pair, pair)
+    points = jnp.broadcast_to(points_ref[...], (1, lane_count))
+    points_row = points.astype(jnp.float32)
+    inverse = 1.0 / points_row
+
+    def factors(first, count, step):
+        place = (first + lax.broadcasted_iota(jnp.int32, (count, lane_count), 0)) * step
+        cosine, sine = turn_cos_sin(turns_of(place.astype(jnp.float32) * wave, points_row, inverse))
+        return jnp.concatenate([cosine, -sine], axis=1)
+
+    near_ref[...] = factors(0, lane_count, 1).astype(jnp.bfloat16)
+    far_ref[...] = factors(0, far_ref.shape[0], lane_count)
+
+    copies[3].wait()
+    rotation = jnp.broadcast_to(coriolis_ref[...], (levels, lane_count))
     lane_wide = lax.broadcasted_iota(jnp.int32, (levels, lane_count), 1)
+    points_wide = jnp.broadcast_to(points, (levels, lane_count))
+    copies[2].wait()
     for block in range(blocks):
         vorticity, spreading, thermal = (
             grid_ref[pl.ds(field * blocks + block, levels, stride=3 * blocks), :]
             for field in range(3)
         )
-        inside = lane_wide < points - block * lane_count
+        inside = lane_wide + block * lane_count < points_wide
         advanced = (
             vorticity - stepsize_delta * (rotation + vorticity) * spreading,
             spreading + stepsize_delta * (rotation * vorticity - spreading * spreading),
             thermal - stepsize_delta * thermal * spreading,
         )
         for field in range(3):
-            rhs_ref[
-                field * levels : (field + 1) * levels,
-                block * lane_count : (block + 1) * lane_count,
-            ] = jnp.where(inside, advanced[field], 0.0).astype(jnp.bfloat16)
-
-    summed = lax.dot_general(
-        table_ref[...],
-        rhs_ref[...],
-        (((1,), (1,)), ((), ())),
-        preferred_element_type=jnp.float32,
-    )
-    wave_ref[:, :channels] = summed
-    scale = jnp.full(tile, weights_ref[0], jnp.float32) / points_vec
+            at = block * channels + field * levels
+            rhs_ref[at : at + levels, :] = jnp.where(inside, advanced[field], 0.0).astype(
+                jnp.bfloat16
+            )
+    partial = jnp.dot(rhs_ref[...], near_ref[...], preferred_element_type=jnp.float32)
+    real = jnp.zeros((channels, lane_count), jnp.float32)
+    imag = jnp.zeros((channels, lane_count), jnp.float32)
+    for block in range(blocks):
+        part_real = partial[block * channels : (block + 1) * channels, :lane_count]
+        part_imag = partial[block * channels : (block + 1) * channels, lane_count:]
+        far_real = far_ref[block : block + 1, :lane_count]
+        far_imag = far_ref[block : block + 1, lane_count:]
+        real = real + (part_real * far_real - part_imag * far_imag)
+        imag = imag + (part_real * far_imag + part_imag * far_real)
+    copies[4].wait()
+    scale = jnp.broadcast_to(weights_ref[...], (1, lane_count)) / points_row
+    half_rows = 2 * per_part
+    for phase, value in enumerate((real, imag)):
+        turned = jnp.pad(value * scale, ((0, lane_count - channels), (0, 0))).T
+        for at in range(half_rows):
+            wave_ref[pl.ds(phase * half_rows + at, sources, stride=piece_rows), :] = turned[
+                at * sources : (at + 1) * sources
+            ]
+
+    copies[5].wait()
     slot_total = highest + 1
     left = lane_count - channels
     for part in range(active):
-        first = jnp.pad(
-            legendre_ref[0, part * per_part].astype(jnp.float32),
-            ((0, 0), (0, lane_count - slot_total)),
-        )
-        second = jnp.pad(
-            legendre_ref[0, part * per_part + 1].astype(jnp.float32),
-            ((0, 0), (0, lane_count - slot_total)),
+        first, second = (
+            jnp.pad(
+                legendre_ref[0, part * per_part + index].astype(jnp.float32),
+                ((0, 0), (0, lane_count - slot_total)),
+            )
+            for index in range(2)
         )
         upper_basis = pltpu.roll(first, channels, 1)
         lower = jnp.where(
@@ -275,11 +300,11 @@
             at = part * group_count + group
             upper = jnp.where(
                 lane < channels,
-                wave_ref[at * piece_rows : (at + 1) * piece_rows, :] * scale,
+                wave_ref[at * piece_rows : (at + 1) * piece_rows, :],
                 upper_basis,
             )
             sent_ref[at] = jnp.concatenate([upper, lower], axis=0).astype(jnp.bfloat16)
-    for at in range(active * group_count, parts * group_count):
+    for at in range(active * group_count, sources):
         sent_ref[at] = jnp.zeros((2 * piece_rows, lane_count), jnp.bfloat16)
 
 
@@ -371,26 +396,48 @@
         ].astype(jnp.bfloat16)
 
 
-def synthesis_kernel(dims, received_ref, table_ref, points_ref, out_ref):
+def synthesis_kernel(
+    dims, received_ref, near_ref, far_ref, points_ref, out_ref, wave_ref, rotated_ref
+):
     levels, lon_count, group_count, slot_count, parts, per_part, highest = dims
+    channels = 3 * levels
     blocks = lon_count // lane_count
     sources = parts * group_count
-    columns = (slot_count // per_part) * group_count * piece_rows
-    pieces = [received_ref[source].astype(jnp.float32) for source in range(sources)]
-    turned = jnp.concatenate(pieces, axis=0).T
-    waves = turned[: 3 * levels, :columns].astype(jnp.bfloat16)
-    points = points_ref[0]
+    half_rows = 2 * per_part
+    for source in range(sources):
+        wave_ref[source * piece_rows : (source + 1) * piece_rows, :] = received_ref[source].astype(
+            jnp.float32
+        )
+    real, imag = (
+        jnp.concatenate(
+            [
+                wave_ref[pl.ds(phase * half_rows + at, sources, stride=piece_rows), :]
+                for at in range(half_rows)
+            ],
+            axis=0,
+        ).T[:channels]
+        for phase in range(2)
+    )
+    for block in range(blocks):
+        far_real = far_ref[block : block + 1, :lane_count]
+        far_imag = far_ref[block : block + 1, lane_count:]
+        rotated_ref[block * channels : (block + 1) * channels, :] = jnp.concatenate(
+            [real * far_real + imag * far_imag, imag * far_real - real * far_imag], axis=1
+        ).astype(jnp.bfloat16)
+    result = lax.dot_general(
+        rotated_ref[...],
+        near_ref[...],
+        (((1,), (1,)), ((), ())),
+        preferred_element_type=jnp.float32,
+    )
     lane_wide = lax.broadcasted_iota(jnp.int32, (levels, lane_count), 1)
-    result = jnp.dot(waves, table_ref[...], preferred_element_type=jnp.float32)
+    points = jnp.broadcast_to(points_ref[...], (levels, lane_count))
     for block in range(blocks):
-        inside = lane_wide < points - block * lane_count
+        inside = lane_wide + block * lane_count < points
         for field in range(3):
-            value = result[
-                field * levels : (field + 1) * levels,
-                block * lane_count : (block + 1) * lane_count,
-            ]
+            at = block * channels + field * levels
             out_ref[pl.ds(field * blocks + block, levels, stride=3 * blocks), :] = jnp.where(
-                inside, value, 0.0
+                inside, result[at : at + levels], 0.0
             )
 
 
@@ -409,30 +456,38 @@
     channels = 3 * levels
     blocks = lon_count // lane_count
     sources = parts * group_count
-    columns = (slot_count // per_part) * group_count * piece_rows
+    far_rows = -(-blocks // piece_rows) * piece_rows
     in_vmem = pl.BlockSpec(memory_space=pltpu.VMEM)
     in_smem = pl.BlockSpec(memory_space=pltpu.SMEM)
-    in_hbm = pl.BlockSpec(memory_space=pl.ANY)
+    in_hbm = pl.BlockSpec(memory_space=pltpu.HBM)
     params = pltpu.CompilerParams(vmem_limit_bytes=16 << 20)
     grid = prognostic_arrays.reshape(channels * blocks, lane_count)
     position = jnp.stack([lax.axis_index("lat"), lax.axis_index("lev")]).astype(jnp.int32)
-    sent, table = pl.pallas_call(
+    points = row_points.reshape(1, 1)
+    basis = jnp.swapaxes(legendre, 2, 3)
+    sent, near, far = pl.pallas_call(
         functools.partial(analysis_kernel, dims),
         name="analysis",
         out_shape=(
             jax.ShapeDtypeStruct((sources, 2 * piece_rows, lane_count), jnp.bfloat16),
-            jax.ShapeDtypeStruct((columns, lon_count), jnp.bfloat16),
+            jax.ShapeDtypeStruct((lane_count, 2 * lane_count), jnp.bfloat16),
+            jax.ShapeDtypeStruct((far_rows, 2 * lane_count), jnp.float32),
         ),
-        in_specs=[in_hbm, in_smem, in_smem, in_smem, in_smem, in_vmem],
-        out_specs=(in_vmem, in_vmem),
+        in_specs=[in_hbm] * 6,
+        out_specs=(in_vmem, in_vmem, in_vmem),
         scratch_shapes=[
-            pltpu.VMEM((channels * blocks, lane_count), jnp.float32),
-            pltpu.VMEM((channels, lon_count), jnp.bfloat16),
-            pltpu.VMEM((columns, lane_count), jnp.float32),
-            pltpu.SemaphoreType.DMA(()),
+            pltpu.VMEM(grid.shape, jnp.float32),
+            pltpu.VMEM((1, 1), jnp.float32),
+            pltpu.VMEM((1, 1), jnp.float32),
+            pltpu.VMEM((1, 1), jnp.int32),
+            pltpu.VMEM(owner_pairs.shape, jnp.int32),
+            pltpu.VMEM(basis.shape, jnp.bfloat16),
+            pltpu.VMEM((blocks * channels, lane_count), jnp.bfloat16),
+            pltpu.VMEM((sources * piece_rows, lane_count), jnp.float32),
+            pltpu.SemaphoreType.DMA((6,)),
         ],
         compiler_params=params,
-    )(grid, coriolis, weights, row_points, owner_pairs, jnp.swapaxes(legendre, 2, 3))
+    )(grid, coriolis.reshape(1, 1), weights.reshape(1, 1), points, owner_pairs, basis)
     received = lax.all_to_all(sent, ("lat", "lev"), split_axis=0, concat_axis=0, tiled=True)
     solved = pl.pallas_call(
         functools.partial(spectral_kernel, dims),
@@ -448,10 +503,14 @@
         functools.partial(synthesis_kernel, dims),
         name="synthesis",
         out_shape=jax.ShapeDtypeStruct((channels * blocks, lane_count), jnp.float32),
-        in_specs=[in_vmem, in_vmem, in_smem],
+        in_specs=[in_vmem] * 4,
         out_specs=in_vmem,
+        scratch_shapes=[
+            pltpu.VMEM((sources * piece_rows, lane_count), jnp.float32),
+            pltpu.VMEM((blocks * channels, 2 * lane_count), jnp.bfloat16),
+        ],
         compiler_params=params,
-    )(returned, table, row_points)
+    )(returned, near, far, points)
     return updated.reshape(prognostic_arrays.shape)
 
 
@@ -468,12 +527,11 @@
         and 4 * per_part == piece_rows
         and slot_count % per_part == 0
         and lon_count % lane_count == 0
-        and lon_count // lane_count <= lane_count
+        and 2 * per_part * parts * group_count == lane_count
         and levels % 16 == 0
         and channels < slot_total <= lane_count
         and 2 * slot_total + channels <= 2 * lane_count
         and lon_count * slot_total < 2**24
-        and (parts * group_count * piece_rows) % lane_count == 0
     )
     arguments = (
         prognostic_arrays, coriolis, weights, row_points, owner_pairs, legendre, depths, diffusion

time: 35.3 us -> 34 us (0.963)
  Pallas kernels: 6.69 us -> 4.68 us
  local copies, waits for them, and re-layouts: 1.75 us -> 2.44 us
    pallas_call x1, Pallas kernels: 3.96 us -> 1.94 us  [packed_body(): pl.pallas_call(functools.partial(analysis_kernel, dims), name='analysis',...]
    unnamed x10, local copies, waits for them, and re-layouts: 1.75 us -> 2.44 us
where the time goes in v2:
time: 34 us; the launch traced here: 33.7 us
  blocking collectives  9.44 us (28%)
  waiting for transfers between devices  7.7 us (23%)
  starting transfers between devices  7.33 us (22%)
  Pallas kernels  4.68 us (14%)
  local copies, waits for them, and re-layouts  2.44 us (7%)
  between operations  2 us (6%)
    all_to_all x1, blocking collectives, packed_body(): lax.all_to_all(solved, ('lat', 'lev'), split_axis=0, concat_axis=0, tiled...  9.44 us
    all_to_all x1, waiting for transfers between devices, packed_body(): lax.all_to_all(sent, ('lat', 'lev'), split_axis=0, concat_axis=0, tiled=T...  7.7 us
    all_to_all x1, starting transfers between devices, packed_body(): lax.all_to_all(sent, ('lat', 'lev'), split_axis=0, concat_axis=0, tiled=T...  7.33 us
    unnamed x10, local copies, waits for them, and re-layouts  2.44 us
    pallas_call x1, Pallas kernels, packed_body(): pl.pallas_call(functools.partial(analysis_kernel, dims), name='analysis',...  1.94 us
    pallas_call x1, Pallas kernels, packed_body(): pl.pallas_call(functools.partial(spectral_kernel, dims), name='spectral',...  1.58 us
    pallas_call x1, Pallas kernels, packed_body(): pl.pallas_call(functools.partial(synthesis_kernel, dims), name='synthesis...  1.16 us
  transfers between devices with their start and end apart: 1, of which 1 were waited for; matrix products, arithmetic and copies ran while one was open for 0% of the time, Pallas kernels for 0%

profile of v2, /device:TPU:0, one launch (start us, length us, event | category | flops | bytes accessed | tf_op | source)
XLA Modules:
  0.0 33.7 jit_solution(8290812308035899102)
XLA Ops:
  1.9 0.0 copy-start.1
  2.0 0.7 %copy-done.1 = s32[8,6]{1,0:T(8,128)S(1)} copy-done((s32[8,6]{1,0:T(8,128)S(1)}, s32[8,6]{1,0:T(8,128)}, u32[]{:S(2)}) %copy-start.1) | copy-done | bytes 216
  2.6 0.0 copy-start
  2.6 1.0 %copy-done = f32[16,3,1,2688]{3,2,1,0:T(1,128)S(1)} copy-done((f32[16,3,1,2688]{3,2,1,0:T(1,128)S(1)}, f32[16,3,1,2688]{3,2,1,0:T(1,128)}, u32[]{:S(2)}) %copy-start) | copy-done | bytes 516120
  3.7 0.0 copy-start.2
  3.7 0.7 %copy-done.2 = bf16[1,6,97,8]{2,3,1,0:T(8,128)(2,1)S(1)} copy-done((bf16[1,6,97,8]{2,3,1,0:T(8,128)(2,1)S(1)}, bf16[1,6,97,8]{2,3,1,0:T(8,128)(2,1)}, u32[]{:S(2)}) %copy-start.2) | copy-done | bytes 9336
  4.4 1.9 %analysis.1 = (bf16[32,16,128]{2,1,0:T(8,128)(2,1)}, bf16[128,256]{1,0:T(8,128)(2,1)S(1)}, f32[24,256]{1,0:T(8,128)S(1)}) custom-call(f32[1008,128]{1,0:T(8,128)S(1)} %bitcast.12, f32[1,1]{1,0:T(1,128)} %bitcast.8.coriolis_hbm, f32[1,1]{1,0:T(1,128)} %bitcast.9.weights_hbm, s32[1,1]{1,0:T(1,128)} %bitcast.10.points_hbm, s32[8,6]{1,0:T(8,128)S(1)} %copy-done.1, ...), custom_call_target="tpu_custom_call" | custom-call | tf_op jit(solution)/shard_map/analysis/pallas_call | solution.py:468
  6.3 7.3 %all-to-all-start = ((bf16[32,16,128]{2,1,0:T(8,128)(2,1)}), bf16[32,16,128]{2,1,0:T(8,128)(2,1)S(1)}, u32[]{:S(2)}, u32[]{:S(2)}) async-start(bf16[32,16,128]{2,1,0:T(8,128)(2,1)} %get-tuple-element.8), calls=%async_computation | async-start | bytes 262144 | tf_op jit(solution)/shard_map/all_to_all | solution.py:491
  13.7 0.0 copy-start.3
  13.7 0.0 copy-start.4
  13.7 0.1 pad_add_fusion.position_ref
  13.8 7.7 %all-to-all-done.received_ref = bf16[32,16,128]{2,1,0:T(8,128)(2,1)S(1)} async-done(((bf16[32,16,128]{2,1,0:T(8,128)(2,1)}), bf16[32,16,128]{2,1,0:T(8,128)(2,1)S(1)}, u32[]{:S(2)}, u32[]{:S(2)}) %all-to-all-start) | async-done | bytes 131104 | tf_op jit(solution)/shard_map/all_to_all | solution.py:491
  21.5 0.0 copy-done.3
  21.5 0.0 copy-done.4
  21.5 1.6 %spectral.1 = bf16[32,8,128]{2,1,0:T(8,128)(2,1)S(1)} custom-call(bf16[32,16,128]{2,1,0:T(8,128)(2,1)S(1)} %all-to-all-done.received_ref, s32[2]{0:T(128)S(1)} %pad_add_fusion.position_ref, s32[8,6]{1,0:T(8,128)S(1)} %copy-done.1, f32[16]{0:T(128)S(1)} %copy-done.3, f32[16]{0:T(128)S(1)} %copy-done.4), custom_call_target="tpu_custom_call" | custom-call | tf_op jit(solution)/shard_map/spectral/pallas_call | solution.py:492
  23.1 9.4 %all_to_all.10.received_ref = bf16[32,8,128]{2,1,0:T(8,128)(2,1)S(1)} all-to-all(bf16[32,8,128]{2,1,0:T(8,128)(2,1)S(1)} %spectral.1), channel_id=1, replica_groups=mesh['lat'=4,'lev'=8] {'lat','lev'}, dimensions={0} | all-to-all | bytes 131072 | tf_op jit(solution)/shard_map/all_to_all | solution.py:501
  32.5 1.2 %synthesis.1 = f32[1008,128]{1,0:T(8,128)} custom-call(bf16[32,8,128]{2,1,0:T(8,128)(2,1)S(1)} %all_to_all.10.received_ref, bf16[128,256]{1,0:T(8,128)(2,1)S(1)} %get-tuple-element.9.near_ref, f32[24,256]{1,0:T(8,128)S(1)} %get-tuple-element.10.far_ref, s32[1,1]{1,0:T(1,128)} %bitcast.11.points_ref), custom_call_target="tpu_custom_call" | custom-call | tf_op jit(solution)/shard_map/synthesis/pallas_call | solution.py:502
Async XLA Ops:
  1.9 0.7 %copy-start.1 = (s32[8,6]{1,0:T(8,128)S(1)}, s32[8,6]{1,0:T(8,128)}, u32[]{:S(2)}) copy-start(s32[8,6]{1,0:T(8,128)} %pairs_ref.1) | copy-start | bytes 580
  2.6 1.0 %copy-start = (f32[16,3,1,2688]{3,2,1,0:T(1,128)S(1)}, f32[16,3,1,2688]{3,2,1,0:T(1,128)}, u32[]{:S(2)}) copy-start(f32[16,3,1,2688]{3,2,1,0:T(1,128)} %param.8) | copy-start | bytes 1548292
  3.7 0.7 %copy-start.2 = (bf16[1,6,97,8]{2,3,1,0:T(8,128)(2,1)S(1)}, bf16[1,6,97,8]{2,3,1,0:T(8,128)(2,1)}, u32[]{:S(2)}) copy-start(bf16[1,6,97,8]{2,3,1,0:T(8,128)(2,1)} %param.13) | copy-start | bytes 27940
  6.3 15.1 %all-to-all-start = ((bf16[32,16,128]{2,1,0:T(8,128)(2,1)}), bf16[32,16,128]{2,1,0:T(8,128)(2,1)S(1)}, u32[]{:S(2)}, u32[]{:S(2)}) async-start(bf16[32,16,128]{2,1,0:T(8,128)(2,1)} %get-tuple-element.8), calls=%async_computation | async-start | bytes 262144 | tf_op jit(solution)/shard_map/all_to_all | solution.py:491
  13.7 7.8 %copy-start.3 = (f32[16]{0:T(128)S(1)}, f32[16]{0:T(128)}, u32[]{:S(2)}) copy-start(f32[16]{0:T(128)} %depths_ref.1) | copy-start | bytes 196
  13.7 7.8 %copy-start.4 = (f32[16]{0:T(128)S(1)}, f32[16]{0:T(128)}, u32[]{:S(2)}) copy-start(f32[16]{0:T(128)} %diffusion_ref.1) | copy-start | bytes 196

commit v3 on v2

--- a/solution.py
+++ b/solution.py
@@ -174,18 +174,15 @@
 def analysis_kernel(
     dims,
     grid_hbm,
-    coriolis_hbm,
-    weights_hbm,
-    points_hbm,
+    coriolis_ref,
+    weights_ref,
+    points_ref,
     pairs_hbm,
     legendre_hbm,
     sent_ref,
     near_ref,
     far_ref,
     grid_ref,
-    coriolis_ref,
-    weights_ref,
-    points_ref,
     pairs_ref,
     legendre_ref,
     rhs_ref,
@@ -202,10 +199,7 @@
         for at, (source, target) in enumerate(
             (
                 (pairs_hbm, pairs_ref),
-                (points_hbm, points_ref),
                 (grid_hbm, grid_ref),
-                (coriolis_hbm, coriolis_ref),
-                (weights_hbm, weights_ref),
                 (legendre_hbm, legendre_ref),
             )
         )
@@ -213,7 +207,6 @@
     for copy in copies:
         copy.start()
     copies[0].wait()
-    copies[1].wait()
 
     tile = (piece_rows, lane_count)
     row = lax.broadcasted_iota(jnp.int32, tile, 0)
@@ -228,7 +221,7 @@
     pair = jnp.sum(spread, axis=0, keepdims=True)
     lane_row = lax.broadcasted_iota(jnp.int32, (1, lane_count), 1)
     wave = jnp.where(lane_row >= per_part * sources, float(highest - 1) - pair, pair)
-    points = jnp.broadcast_to(points_ref[...], (1, lane_count))
+    points = jnp.full((1, lane_count), points_ref[0], jnp.int32)
     points_row = points.astype(jnp.float32)
     inverse = 1.0 / points_row
 
@@ -240,11 +233,10 @@
     near_ref[...] = factors(0, lane_count, 1).astype(jnp.bfloat16)
     far_ref[...] = factors(0, far_ref.shape[0], lane_count)
 
-    copies[3].wait()
-    rotation = jnp.broadcast_to(coriolis_ref[...], (levels, lane_count))
+    rotation = coriolis_ref[0]
     lane_wide = lax.broadcasted_iota(jnp.int32, (levels, lane_count), 1)
     points_wide = jnp.broadcast_to(points, (levels, lane_count))
-    copies[2].wait()
+    copies[1].wait()
     for block in range(blocks):
         vorticity, spreading, thermal = (
             grid_ref[pl.ds(field * blocks + block, levels, stride=3 * blocks), :]
@@ -271,8 +263,7 @@
         far_imag = far_ref[block : block + 1, lane_count:]
         real = real + (part_real * far_real - part_imag * far_imag)
         imag = imag + (part_real * far_imag + part_imag * far_real)
-    copies[4].wait()
-    scale = jnp.broadcast_to(weights_ref[...], (1, lane_count)) / points_row
+    scale = jnp.full((1, lane_count), weights_ref[0], jnp.float32) / points_row
     half_rows = 2 * per_part
     for phase, value in enumerate((real, imag)):
         turned = jnp.pad(value * scale, ((0, lane_count - channels), (0, 0))).T
@@ -281,7 +272,7 @@
                 at * sources : (at + 1) * sources
             ]
 
-    copies[5].wait()
+    copies[2].wait()
     slot_total = highest + 1
     left = lane_count - channels
     for part in range(active):
@@ -431,7 +422,7 @@
         preferred_element_type=jnp.float32,
     )
     lane_wide = lax.broadcasted_iota(jnp.int32, (levels, lane_count), 1)
-    points = jnp.broadcast_to(points_ref[...], (levels, lane_count))
+    points = points_ref[0]
     for block in range(blocks):
         inside = lane_wide + block * lane_count < points
         for field in range(3):
@@ -463,7 +454,6 @@
     params = pltpu.CompilerParams(vmem_limit_bytes=16 << 20)
     grid = prognostic_arrays.reshape(channels * blocks, lane_count)
     position = jnp.stack([lax.axis_index("lat"), lax.axis_index("lev")]).astype(jnp.int32)
-    points = row_points.reshape(1, 1)
     basis = jnp.swapaxes(legendre, 2, 3)
     sent, near, far = pl.pallas_call(
         functools.partial(analysis_kernel, dims),
@@ -473,21 +463,18 @@
             jax.ShapeDtypeStruct((lane_count, 2 * lane_count), jnp.bfloat16),
             jax.ShapeDtypeStruct((far_rows, 2 * lane_count), jnp.float32),
         ),
-        in_specs=[in_hbm] * 6,
+        in_specs=[in_hbm, in_smem, in_smem, in_smem, in_hbm, in_hbm],
         out_specs=(in_vmem, in_vmem, in_vmem),
         scratch_shapes=[
             pltpu.VMEM(grid.shape, jnp.float32),
-            pltpu.VMEM((1, 1), jnp.float32),
-            pltpu.VMEM((1, 1), jnp.float32),
-            pltpu.VMEM((1, 1), jnp.int32),
             pltpu.VMEM(owner_pairs.shape, jnp.int32),
             pltpu.VMEM(basis.shape, jnp.bfloat16),
             pltpu.VMEM((blocks * channels, lane_count), jnp.bfloat16),
             pltpu.VMEM((sources * piece_rows, lane_count), jnp.float32),
-            pltpu.SemaphoreType.DMA((6,)),
+            pltpu.SemaphoreType.DMA((3,)),
         ],
-        compiler_params=params,
-    )(grid, coriolis.reshape(1, 1), weights.reshape(1, 1), points, owner_pairs, basis)
+        compiler_params=pltpu.CompilerParams(vmem_limit_bytes=67043328),
+    )(grid, coriolis, weights, row_points, owner_pairs, basis)
     received = lax.all_to_all(sent, ("lat", "lev"), split_axis=0, concat_axis=0, tiled=True)
     solved = pl.pallas_call(
         functools.partial(spectral_kernel, dims),
@@ -503,14 +490,14 @@
         functools.partial(synthesis_kernel, dims),
         name="synthesis",
         out_shape=jax.ShapeDtypeStruct((channels * blocks, lane_count), jnp.float32),
-        in_specs=[in_vmem] * 4,
+        in_specs=[in_vmem, in_vmem, in_vmem, in_smem],
         out_specs=in_vmem,
         scratch_shapes=[
             pltpu.VMEM((sources * piece_rows, lane_count), jnp.float32),
             pltpu.VMEM((blocks * channels, 2 * lane_count), jnp.bfloat16),
         ],
         compiler_params=params,
-    )(returned, near, far, points)
+    )(returned, near, far, row_points)
     return updated.reshape(prognostic_arrays.shape)
 
 

time: 34 us -> 31.8 us (0.935)
  local copies, waits for them, and re-layouts: 2.44 us -> 0.03 us
    unnamed x10, local copies, waits for them, and re-layouts: 2.44 us -> 0.03 us
where the time goes in v3:
time: 31.8 us; the launch traced here: 31.6 us
  blocking collectives  9.44 us (30%)
  waiting for transfers between devices  7.69 us (24%)
  starting transfers between devices  7.33 us (23%)
  Pallas kernels  4.99 us (16%)
  between operations  2.02 us (6%)
    all_to_all x1, blocking collectives, packed_body(): lax.all_to_all(solved, ('lat', 'lev'), split_axis=0, concat_axis=0, tiled...  9.44 us
    all_to_all x1, waiting for transfers between devices, packed_body(): lax.all_to_all(sent, ('lat', 'lev'), split_axis=0, concat_axis=0, tiled=T...  7.69 us
    all_to_all x1, starting transfers between devices, packed_body(): lax.all_to_all(sent, ('lat', 'lev'), split_axis=0, concat_axis=0, tiled=T...  7.33 us
    pallas_call x1, Pallas kernels, packed_body(): pl.pallas_call(functools.partial(analysis_kernel, dims), name='analysis',...  2.24 us
    pallas_call x1, Pallas kernels, packed_body(): pl.pallas_call(functools.partial(spectral_kernel, dims), name='spectral',...  1.58 us
    pallas_call x1, Pallas kernels, packed_body(): pl.pallas_call(functools.partial(synthesis_kernel, dims), name='synthesis...  1.16 us
  transfers between devices with their start and end apart: 1, of which 1 were waited for; matrix products, arithmetic and copies ran while one was open for 0% of the time, Pallas kernels for 0%

profile of v3, /device:TPU:0, one launch (start us, length us, event | category | flops | bytes accessed | tf_op | source)
XLA Modules:
  0.0 31.6 jit_solution(10408593018618379592)
XLA Ops:
  1.9 2.2 %analysis.1 = (bf16[32,16,128]{2,1,0:T(8,128)(2,1)}, bf16[128,256]{1,0:T(8,128)(2,1)}, f32[24,256]{1,0:T(8,128)}) custom-call(f32[1008,128]{1,0:T(8,128)} %bitcast.5, f32[1]{0:T(128)S(6)} %copy.11.coriolis_ref, f32[1]{0:T(128)S(6)} %copy.12.weights_ref, s32[1]{0:T(128)S(6)} %copy.13.points_ref, s32[8,6]{1,0:T(8,128)} %pairs_ref.1, bf16[1,6,8,97]{3,2,1,0:T(8,128)(2,1)} %bitcast.6), custom_call_target="tpu_custom_call" | custom-call | tf_op jit(solution)/shard_map/analysis/pallas_call | solution.py:458
  4.2 7.3 %all-to-all-start = ((bf16[32,16,128]{2,1,0:T(8,128)(2,1)}), bf16[32,16,128]{2,1,0:T(8,128)(2,1)S(1)}, u32[]{:S(2)}, u32[]{:S(2)}) async-start(bf16[32,16,128]{2,1,0:T(8,128)(2,1)} %get-tuple-element.8), calls=%async_computation | async-start | bytes 262144 | tf_op jit(solution)/shard_map/all_to_all | solution.py:478
  11.5 0.0 copy-start.2
  11.6 0.0 copy-start.3
  11.6 0.0 copy-start.4
  11.6 0.1 pad_add_fusion.position_ref
  11.7 7.7 %all-to-all-done.received_ref = bf16[32,16,128]{2,1,0:T(8,128)(2,1)S(1)} async-done(((bf16[32,16,128]{2,1,0:T(8,128)(2,1)}), bf16[32,16,128]{2,1,0:T(8,128)(2,1)S(1)}, u32[]{:S(2)}, u32[]{:S(2)}) %all-to-all-start) | async-done | bytes 131104 | tf_op jit(solution)/shard_map/all_to_all | solution.py:478
  19.3 0.0 copy-done.2
  19.3 0.0 copy-done.3
  19.3 0.0 copy-done.4
  19.4 1.6 %spectral.1 = bf16[32,8,128]{2,1,0:T(8,128)(2,1)S(1)} custom-call(bf16[32,16,128]{2,1,0:T(8,128)(2,1)S(1)} %all-to-all-done.received_ref, s32[2]{0:T(128)S(1)} %pad_add_fusion.position_ref, s32[8,6]{1,0:T(8,128)S(1)} %copy-done.2, f32[16]{0:T(128)S(1)} %copy-done.3, f32[16]{0:T(128)S(1)} %copy-done.4), custom_call_target="tpu_custom_call" | custom-call | tf_op jit(solution)/shard_map/spectral/pallas_call | solution.py:479
  20.9 0.0 copy-start
  21.0 0.0 copy-start.1
  21.0 9.4 %all_to_all.10.received_ref = bf16[32,8,128]{2,1,0:T(8,128)(2,1)S(1)} all-to-all(bf16[32,8,128]{2,1,0:T(8,128)(2,1)S(1)} %spectral.1), channel_id=1, replica_groups=mesh['lat'=4,'lev'=8] {'lat','lev'}, dimensions={0} | all-to-all | bytes 131072 | tf_op jit(solution)/shard_map/all_to_all | solution.py:488
  30.4 0.0 copy-done
  30.4 0.0 copy-done.1
  30.4 1.2 %synthesis.1 = f32[1008,128]{1,0:T(8,128)} custom-call(bf16[32,8,128]{2,1,0:T(8,128)(2,1)S(1)} %all_to_all.10.received_ref, bf16[128,256]{1,0:T(8,128)(2,1)S(1)} %copy-done, f32[24,256]{1,0:T(8,128)S(1)} %copy-done.1, s32[1]{0:T(128)S(6)} %copy.13.points_ref), custom_call_target="tpu_custom_call" | custom-call | tf_op jit(solution)/shard_map/synthesis/pallas_call | solution.py:489
Async XLA Ops:
  4.2 15.1 %all-to-all-start = ((bf16[32,16,128]{2,1,0:T(8,128)(2,1)}), bf16[32,16,128]{2,1,0:T(8,128)(2,1)S(1)}, u32[]{:S(2)}, u32[]{:S(2)}) async-start(bf16[32,16,128]{2,1,0:T(8,128)(2,1)} %get-tuple-element.8), calls=%async_computation | async-start | bytes 262144 | tf_op jit(solution)/shard_map/all_to_all | solution.py:478
  11.5 7.8 %copy-start.2 = (s32[8,6]{1,0:T(8,128)S(1)}, s32[8,6]{1,0:T(8,128)}, u32[]{:S(2)}) copy-start(s32[8,6]{1,0:T(8,128)} %pairs_ref.1) | copy-start | bytes 580
  11.6 7.8 %copy-start.3 = (f32[16]{0:T(128)S(1)}, f32[16]{0:T(128)}, u32[]{:S(2)}) copy-start(f32[16]{0:T(128)} %depths_ref.1) | copy-start | bytes 196
  11.6 7.8 %copy-start.4 = (f32[16]{0:T(128)S(1)}, f32[16]{0:T(128)}, u32[]{:S(2)}) copy-start(f32[16]{0:T(128)} %diffusion_ref.1) | copy-start | bytes 196
  20.9 9.5 %copy-start = (bf16[128,256]{1,0:T(8,128)(2,1)S(1)}, bf16[128,256]{1,0:T(8,128)(2,1)}, u32[]{:S(2)}) copy-start(bf16[128,256]{1,0:T(8,128)(2,1)} %get-tuple-element.9.near_ref) | copy-start | bytes 196612
  21.0 9.5 %copy-start.1 = (f32[24,256]{1,0:T(8,128)S(1)}, f32[24,256]{1,0:T(8,128)}, u32[]{:S(2)}) copy-start(f32[24,256]{1,0:T(8,128)} %get-tuple-element.10.far_ref) | copy-start | bytes 73732

commit v4 on v2

--- a/solution.py
+++ b/solution.py
@@ -228,7 +228,7 @@
     pair = jnp.sum(spread, axis=0, keepdims=True)
     lane_row = lax.broadcasted_iota(jnp.int32, (1, lane_count), 1)
     wave = jnp.where(lane_row >= per_part * sources, float(highest - 1) - pair, pair)
-    points = jnp.broadcast_to(points_ref[...], (1, lane_count))
+    points = jnp.full((1, lane_count), points_ref[0], jnp.int32)
     points_row = points.astype(jnp.float32)
     inverse = 1.0 / points_row
 
@@ -241,7 +241,7 @@
     far_ref[...] = factors(0, far_ref.shape[0], lane_count)
 
     copies[3].wait()
-    rotation = jnp.broadcast_to(coriolis_ref[...], (levels, lane_count))
+    rotation = coriolis_ref[0]
     lane_wide = lax.broadcasted_iota(jnp.int32, (levels, lane_count), 1)
     points_wide = jnp.broadcast_to(points, (levels, lane_count))
     copies[2].wait()
@@ -272,7 +272,7 @@
         real = real + (part_real * far_real - part_imag * far_imag)
         imag = imag + (part_real * far_imag + part_imag * far_real)
     copies[4].wait()
-    scale = jnp.broadcast_to(weights_ref[...], (1, lane_count)) / points_row
+    scale = jnp.full((1, lane_count), weights_ref[0], jnp.float32) / points_row
     half_rows = 2 * per_part
     for phase, value in enumerate((real, imag)):
         turned = jnp.pad(value * scale, ((0, lane_count - channels), (0, 0))).T
@@ -431,7 +431,7 @@
         preferred_element_type=jnp.float32,
     )
     lane_wide = lax.broadcasted_iota(jnp.int32, (levels, lane_count), 1)
-    points = jnp.broadcast_to(points_ref[...], (levels, lane_count))
+    points = points_ref[0]
     for block in range(blocks):
         inside = lane_wide + block * lane_count < points
         for field in range(3):
@@ -463,31 +463,42 @@
     params = pltpu.CompilerParams(vmem_limit_bytes=16 << 20)
     grid = prognostic_arrays.reshape(channels * blocks, lane_count)
     position = jnp.stack([lax.axis_index("lat"), lax.axis_index("lev")]).astype(jnp.int32)
-    points = row_points.reshape(1, 1)
     basis = jnp.swapaxes(legendre, 2, 3)
-    sent, near, far = pl.pallas_call(
+    analysis_shapes = (
+        jax.ShapeDtypeStruct((sources, 2 * piece_rows, lane_count), jnp.bfloat16),
+        jax.ShapeDtypeStruct((lane_count, 2 * lane_count), jnp.bfloat16),
+        jax.ShapeDtypeStruct((far_rows, 2 * lane_count), jnp.float32),
+    )
+    analysis = pl.pallas_call(
         functools.partial(analysis_kernel, dims),
         name="analysis",
-        out_shape=(
-            jax.ShapeDtypeStruct((sources, 2 * piece_rows, lane_count), jnp.bfloat16),
-            jax.ShapeDtypeStruct((lane_count, 2 * lane_count), jnp.bfloat16),
-            jax.ShapeDtypeStruct((far_rows, 2 * lane_count), jnp.float32),
-        ),
+        out_shape=analysis_shapes,
         in_specs=[in_hbm] * 6,
         out_specs=(in_vmem, in_vmem, in_vmem),
         scratch_shapes=[
             pltpu.VMEM(grid.shape, jnp.float32),
-            pltpu.VMEM((1, 1), jnp.float32),
-            pltpu.VMEM((1, 1), jnp.float32),
-            pltpu.VMEM((1, 1), jnp.int32),
+            pltpu.SMEM((1,), jnp.float32),
+            pltpu.SMEM((1,), jnp.float32),
+            pltpu.SMEM((1,), jnp.int32),
             pltpu.VMEM(owner_pairs.shape, jnp.int32),
             pltpu.VMEM(basis.shape, jnp.bfloat16),
             pltpu.VMEM((blocks * channels, lane_count), jnp.bfloat16),
             pltpu.VMEM((sources * piece_rows, lane_count), jnp.float32),
             pltpu.SemaphoreType.DMA((6,)),
         ],
-        compiler_params=params,
-    )(grid, coriolis.reshape(1, 1), weights.reshape(1, 1), points, owner_pairs, basis)
+        compiler_params=pltpu.CompilerParams(vmem_limit_bytes=67043328),
+    )
+    sent, near, far = lax.cond(
+        position[0] >= 0,
+        lambda *inputs: tuple(analysis(*inputs)),
+        lambda *inputs: tuple(jnp.zeros(made.shape, made.dtype) for made in analysis_shapes),
+        grid,
+        coriolis,
+        weights,
+        row_points,
+        owner_pairs,
+        basis,
+    )
     received = lax.all_to_all(sent, ("lat", "lev"), split_axis=0, concat_axis=0, tiled=True)
     solved = pl.pallas_call(
         functools.partial(spectral_kernel, dims),
@@ -503,14 +514,14 @@
         functools.partial(synthesis_kernel, dims),
         name="synthesis",
         out_shape=jax.ShapeDtypeStruct((channels * blocks, lane_count), jnp.float32),
-        in_specs=[in_vmem] * 4,
+        in_specs=[in_vmem, in_vmem, in_vmem, in_smem],
         out_specs=in_vmem,
         scratch_shapes=[
             pltpu.VMEM((sources * piece_rows, lane_count), jnp.float32),
             pltpu.VMEM((blocks * channels, 2 * lane_count), jnp.bfloat16),
         ],
         compiler_params=params,
-    )(returned, near, far, points)
+    )(returned, near, far, row_points)
     return updated.reshape(prognostic_arrays.shape)
 
 

time: 34 us -> 33.8 us (level)
  blocking collectives: 9.44 us -> 0 us
  waiting for transfers between devices: 7.7 us -> 14.3 us
  Pallas kernels: 4.68 us -> 8.43 us
  starting transfers between devices: 7.33 us -> 9.9 us
  local copies, waits for them, and re-layouts: 2.44 us -> 0.02 us
  between operations: 2 us -> 0.71 us
    all_to_all x1 -> x0, blocking collectives: 9.44 us -> none  [packed_body(): lax.all_to_all(solved, ('lat', 'lev'), split_axis=0, concat_axis=0, tiled...]
    all_to_all x0 -> x1, waiting for transfers between devices: none -> 6.63 us  [packed_body(): lax.all_to_all(solved, ('lat', 'lev'), split_axis=0, concat_axis=0, tiled...]
    all_to_all x0 -> x1, starting transfers between devices: none -> 2.57 us  [packed_body(): lax.all_to_all(solved, ('lat', 'lev'), split_axis=0, concat_axis=0, tiled...]
    unnamed x10 -> x6, local copies, waits for them, and re-layouts: 2.44 us -> 0.02 us
    pallas_call x1, Pallas kernels: 1.94 us -> 4.22 us  [packed_body(): analysis(*inputs)]
    pallas_call x1, Pallas kernels: 1.16 us -> 2 us  [packed_body(): pl.pallas_call(functools.partial(synthesis_kernel, dims), name='synthesis...]
    pallas_call x1, Pallas kernels: 1.58 us -> 2.21 us  [packed_body(): pl.pallas_call(functools.partial(spectral_kernel, dims), name='spectral',...]
  transfers between devices with their start and end apart: 1 -> 2, of which waited for: 1 -> 2; matrix products, arithmetic and copies ran while one was open for 0% -> 0% of each run, Pallas kernels for 0% -> 0%
where the time goes in v4:
time: 33.8 us; the launch traced here: 33.5 us
  waiting for transfers between devices  14.3 us (42%)
  starting transfers between devices  9.9 us (29%)
  Pallas kernels  8.43 us (25%)
  between operations  0.71 us (2%)
    all_to_all x1, waiting for transfers between devices, packed_body(): lax.all_to_all(sent, ('lat', 'lev'), split_axis=0, concat_axis=0, tiled=T...  7.69 us
    all_to_all x1, starting transfers between devices, packed_body(): lax.all_to_all(sent, ('lat', 'lev'), split_axis=0, concat_axis=0, tiled=T...  7.33 us
    all_to_all x1, waiting for transfers between devices, packed_body(): lax.all_to_all(solved, ('lat', 'lev'), split_axis=0, concat_axis=0, tiled...  6.63 us
    pallas_call x1, Pallas kernels, packed_body(): analysis(*inputs)  4.22 us
    all_to_all x1, starting transfers between devices, packed_body(): lax.all_to_all(solved, ('lat', 'lev'), split_axis=0, concat_axis=0, tiled...  2.57 us
    pallas_call x1, Pallas kernels, packed_body(): pl.pallas_call(functools.partial(spectral_kernel, dims), name='spectral',...  2.21 us
    pallas_call x1, Pallas kernels, packed_body(): pl.pallas_call(functools.partial(synthesis_kernel, dims), name='synthesis...  2 us
  transfers between devices with their start and end apart: 2, of which 2 were waited for; matrix products, arithmetic and copies ran while one was open for 0% of the time, Pallas kernels for 0%

profile of v4, /device:TPU:0, one launch (start us, length us, event | category | flops | bytes accessed | tf_op | source)
XLA Modules:
  0.0 33.5 jit_solution(1186853282270860361)
XLA Ops:
  0.0 4.2 %conditional.1 = ((bf16[32,16,128]{2,1,0:T(8,128)(2,1)}, bf16[128,256]{1,0:T(8,128)(2,1)}, f32[24,256]{1,0:T(8,128)})) conditional(s32[]{:T(128)} %convert_element_type.3, () %tuple.12, (f32[16,3,1,2688]{3,2,1,0:T(1,128)}, f32[1]{0:T(128)}, f32[1]{0:T(128)}, s32[1]{0:T(128)}, s32[8,6]{1,0:T(8,128)}, /*index=5*/bf16[1,6,8,97]{3,2,1,0:T(8,128)(2,1)}) %tuple.20), branch_computations={%region_0.0_spmd, %region_1.0_spmd} | conditional | bytes 221224 | solution.py:491
  0.0 4.2 %analysis.1 = (bf16[32,16,128]{2,1,0:T(8,128)(2,1)}, bf16[128,256]{1,0:T(8,128)(2,1)}, f32[24,256]{1,0:T(8,128)}) custom-call(f32[1008,128]{1,0:T(8,128)} %bitcast.5, f32[1]{0:T(128)} %get-tuple-element.34.coriolis_hbm, f32[1]{0:T(128)} %get-tuple-element.35.weights_hbm, s32[1]{0:T(128)} %get-tuple-element.21.points_hbm, ...), custom_call_target="tpu_custom_call" | custom-call | tf_op jit(solution)/shard_map/cond/branch_1_fun/analysis/pallas_call | solution.py:493
  4.2 7.3 %all-to-all-start = ((bf16[32,16,128]{2,1,0:T(8,128)(2,1)}), bf16[32,16,128]{2,1,0:T(8,128)(2,1)S(1)}, u32[]{:S(2)}, u32[]{:S(2)}) async-start(bf16[32,16,128]{2,1,0:T(8,128)(2,1)} %get-tuple-element.27), calls=%async_computation | async-start | bytes 262144 | tf_op jit(solution)/shard_map/all_to_all | solution.py:502
  11.6 0.0 copy-start.2
  11.6 0.0 copy-start
  11.6 0.0 copy-start.1
  11.6 0.1 pad_add_fusion.position_ref
  11.7 7.7 %all-to-all-done.received_ref = bf16[32,16,128]{2,1,0:T(8,128)(2,1)S(1)} async-done(((bf16[32,16,128]{2,1,0:T(8,128)(2,1)}), bf16[32,16,128]{2,1,0:T(8,128)(2,1)S(1)}, u32[]{:S(2)}, u32[]{:S(2)}) %all-to-all-start) | async-done | bytes 131104 | tf_op jit(solution)/shard_map/all_to_all | solution.py:502
  19.4 0.0 copy-done.2
  19.4 0.0 copy-done
  19.4 0.0 copy-done.1
  19.4 2.2 %spectral.1 = bf16[32,8,128]{2,1,0:T(8,128)(2,1)} custom-call(bf16[32,16,128]{2,1,0:T(8,128)(2,1)S(1)} %all-to-all-done.received_ref, s32[2]{0:T(128)S(1)} %pad_add_fusion.position_ref, s32[8,6]{1,0:T(8,128)S(1)} %copy-done.2, f32[16]{0:T(128)S(1)} %copy-done, f32[16]{0:T(128)S(1)} %copy-done.1), custom_call_target="tpu_custom_call" | custom-call | tf_op jit(solution)/shard_map/spectral/pallas_call | solution.py:503
  21.6 2.6 %all-to-all-start.1 = ((bf16[32,8,128]{2,1,0:T(8,128)(2,1)}), bf16[32,8,128]{2,1,0:T(8,128)(2,1)S(1)}, u32[]{:S(2)}, u32[]{:S(2)}) async-start(bf16[32,8,128]{2,1,0:T(8,128)(2,1)} %spectral.1), calls=%async_computation.1 | async-start | bytes 131072 | tf_op jit(solution)/shard_map/all_to_all | solution.py:512
  24.8 6.6 %all-to-all-done.1.received_ref = bf16[32,8,128]{2,1,0:T(8,128)(2,1)S(1)} async-done(((bf16[32,8,128]{2,1,0:T(8,128)(2,1)}), bf16[32,8,128]{2,1,0:T(8,128)(2,1)S(1)}, u32[]{:S(2)}, u32[]{:S(2)}) %all-to-all-start.1) | async-done | bytes 65568 | tf_op jit(solution)/shard_map/all_to_all | solution.py:512
  31.5 2.0 %synthesis.1 = f32[1008,128]{1,0:T(8,128)} custom-call(bf16[32,8,128]{2,1,0:T(8,128)(2,1)S(1)} %all-to-all-done.1.received_ref, bf16[128,256]{1,0:T(8,128)(2,1)} %get-tuple-element.28.near_ref, f32[24,256]{1,0:T(8,128)} %get-tuple-element.29.far_ref, s32[1]{0:T(128)S(6)} %copy.22.points_ref), custom_call_target="tpu_custom_call" | custom-call | tf_op jit(solution)/shard_map/synthesis/pallas_call | solution.py:513
Async XLA Ops:
  4.2 15.1 %all-to-all-start = ((bf16[32,16,128]{2,1,0:T(8,128)(2,1)}), bf16[32,16,128]{2,1,0:T(8,128)(2,1)S(1)}, u32[]{:S(2)}, u32[]{:S(2)}) async-start(bf16[32,16,128]{2,1,0:T(8,128)(2,1)} %get-tuple-element.27), calls=%async_computation | async-start | bytes 262144 | tf_op jit(solution)/shard_map/all_to_all | solution.py:502
  11.6 7.8 %copy-start.2 = (s32[8,6]{1,0:T(8,128)S(1)}, s32[8,6]{1,0:T(8,128)}, u32[]{:S(2)}) copy-start(s32[8,6]{1,0:T(8,128)} %pairs_ref.1) | copy-start | bytes 580
  11.6 7.8 %copy-start = (f32[16]{0:T(128)S(1)}, f32[16]{0:T(128)}, u32[]{:S(2)}) copy-start(f32[16]{0:T(128)} %depths_ref.1) | copy-start | bytes 196
  11.6 7.8 %copy-start.1 = (f32[16]{0:T(128)S(1)}, f32[16]{0:T(128)}, u32[]{:S(2)}) copy-start(f32[16]{0:T(128)} %diffusion_ref.1) | copy-start | bytes 196
  21.6 9.9 %all-to-all-start.1 = ((bf16[32,8,128]{2,1,0:T(8,128)(2,1)}), bf16[32,8,128]{2,1,0:T(8,128)(2,1)S(1)}, u32[]{:S(2)}, u32[]{:S(2)}) async-start(bf16[32,8,128]{2,1,0:T(8,128)(2,1)} %spectral.1), calls=%async_computation.1 | async-start | bytes 131072 | tf_op jit(solution)/shard_map/all_to_all | solution.py:512

commit v5 on v3

--- a/solution.py
+++ b/solution.py
@@ -171,6 +171,37 @@
     return rest * inverse
 
 
+def wave_row(dims, pairs):
+    levels, lon_count, group_count, slot_count, parts, per_part, highest = dims
+    sources = parts * group_count
+    tile = (piece_rows, lane_count)
+    row = lax.broadcasted_iota(jnp.int32, tile, 0)
+    lane = lax.broadcasted_iota(jnp.int32, tile, 1)
+    lane_slot = lane // group_count % parts * per_part + lane // sources % per_part
+    at_group = lane % group_count == row
+    spread = jnp.zeros(tile, jnp.float32)
+    for slot in range(slot_count):
+        chosen = jnp.logical_and(at_group, lane_slot == slot)
+        spread = jnp.where(chosen, pairs[:, slot : slot + 1].astype(jnp.float32), spread)
+    pair = jnp.sum(spread, axis=0, keepdims=True)
+    lane_row = lax.broadcasted_iota(jnp.int32, (1, lane_count), 1)
+    return jnp.where(lane_row >= per_part * sources, float(highest - 1) - pair, pair)
+
+
+def factors(count, step, wave, points_row):
+    place = lax.broadcasted_iota(jnp.int32, (count, lane_count), 0) * step
+    cosine, sine = turn_cos_sin(
+        turns_of(place.astype(jnp.float32) * wave, points_row, 1.0 / points_row)
+    )
+    return jnp.concatenate([cosine, -sine], axis=1)
+
+
+def pair_rows(units):
+    if len(units) % 2:
+        units = units + [jnp.zeros_like(units[0])]
+    return [jnp.concatenate(units[at : at + 2], axis=0) for at in range(0, len(units), 2)]
+
+
 def analysis_kernel(
     dims,
     grid_hbm,
@@ -180,11 +211,11 @@
     pairs_hbm,
     legendre_hbm,
     sent_ref,
-    near_ref,
-    far_ref,
     grid_ref,
     pairs_ref,
     legendre_ref,
+    near_ref,
+    far_ref,
     rhs_ref,
     wave_ref,
     sems,
@@ -194,85 +225,84 @@
     blocks = lon_count // lane_count
     active = slot_count // per_part
     sources = parts * group_count
-    copies = [
-        pltpu.make_async_copy(source, target, sems.at[at])
-        for at, (source, target) in enumerate(
-            (
-                (pairs_hbm, pairs_ref),
-                (grid_hbm, grid_ref),
-                (legendre_hbm, legendre_ref),
-            )
+    level_rows = 3 * blocks
+    chunks = levels // piece_rows
+    chunk_rows = piece_rows * level_rows
+    copies = [pltpu.make_async_copy(pairs_hbm, pairs_ref, sems.at[0])]
+    for chunk in range(chunks):
+        rows = pl.ds(chunk * chunk_rows, chunk_rows)
+        copies.append(
+            pltpu.make_async_copy(grid_hbm.at[rows], grid_ref.at[rows], sems.at[1 + chunk])
         )
-    ]
+    copies.append(pltpu.make_async_copy(legendre_hbm, legendre_ref, sems.at[1 + chunks]))
     for copy in copies:
         copy.start()
     copies[0].wait()
 
+    points = points_ref[0]
+    points_row = jnp.full((1, lane_count), points, jnp.int32).astype(jnp.float32)
+    wave = wave_row(dims, pairs_ref[...])
+    near_ref[...] = factors(lane_count, 1, wave, points_row).astype(jnp.bfloat16)
+    far_ref[...] = factors(far_ref.shape[0], lane_count, wave, points_row)
+    rotation = coriolis_ref[0]
     tile = (piece_rows, lane_count)
-    row = lax.broadcasted_iota(jnp.int32, tile, 0)
     lane = lax.broadcasted_iota(jnp.int32, tile, 1)
-    lane_slot = lane // group_count % parts * per_part + lane // sources % per_part
-    at_group = lane % group_count == row
-    pairs = pairs_ref[...].astype(jnp.float32)
-    spread = jnp.zeros(tile, jnp.float32)
-    for slot in range(slot_count):
-        chosen = jnp.logical_and(at_group, lane_slot == slot)
-        spread = jnp.where(chosen, pairs[:, slot : slot + 1], spread)
-    pair = jnp.sum(spread, axis=0, keepdims=True)
-    lane_row = lax.broadcasted_iota(jnp.int32, (1, lane_count), 1)
-    wave = jnp.where(lane_row >= per_part * sources, float(highest - 1) - pair, pair)
-    points = jnp.full((1, lane_count), points_ref[0], jnp.int32)
-    points_row = points.astype(jnp.float32)
-    inverse = 1.0 / points_row
-
-    def factors(first, count, step):
-        place = (first + lax.broadcasted_iota(jnp.int32, (count, lane_count), 0)) * step
-        cosine, sine = turn_cos_sin(turns_of(place.astype(jnp.float32) * wave, points_row, inverse))
-        return jnp.concatenate([cosine, -sine], axis=1)
-
-    near_ref[...] = factors(0, lane_count, 1).astype(jnp.bfloat16)
-    far_ref[...] = factors(0, far_ref.shape[0], lane_count)
-
-    rotation = coriolis_ref[0]
-    lane_wide = lax.broadcasted_iota(jnp.int32, (levels, lane_count), 1)
-    points_wide = jnp.broadcast_to(points, (levels, lane_count))
-    copies[1].wait()
-    for block in range(blocks):
-        vorticity, spreading, thermal = (
-            grid_ref[pl.ds(field * blocks + block, levels, stride=3 * blocks), :]
-            for field in range(3)
-        )
-        inside = lane_wide + block * lane_count < points_wide
-        advanced = (
-            vorticity - stepsize_delta * (rotation + vorticity) * spreading,
-            spreading + stepsize_delta * (rotation * vorticity - spreading * spreading),
-            thermal - stepsize_delta * thermal * spreading,
+    padded = (level_rows + level_rows % 2) * piece_rows
+    real = [None] * (3 * chunks)
+    imag = [None] * (3 * chunks)
+    for chunk in range(chunks):
+        copies[1 + chunk].wait()
+        units = []
+        for field in range(3):
+            for block in range(blocks):
+
+                def load(which):
+                    at = chunk * chunk_rows + which * blocks + block
+                    return grid_ref[pl.ds(at, piece_rows, stride=level_rows), :]
+
+                spreading = load(1)
+                if field == 0:
+                    vorticity = load(0)
+                    value = vorticity - stepsize_delta * (rotation + vorticity) * spreading
+                elif field == 1:
+                    value = spreading + stepsize_delta * (
+                        rotation * load(0) - spreading * spreading
+                    )
+                else:
+                    thermal = load(2)
+                    value = thermal - stepsize_delta * thermal * spreading
+                units.append(jnp.where(lane < points - block * lane_count, value, 0.0))
+        for at, two in enumerate(pair_rows(units)):
+            start = chunk * padded + at * 2 * piece_rows
+            rhs_ref[start : start + 2 * piece_rows, :] = two.astype(jnp.bfloat16)
+        partial = jnp.dot(
+            rhs_ref[chunk * padded : (chunk + 1) * padded, :],
+            near_ref[...],
+            preferred_element_type=jnp.float32,
         )
         for field in range(3):
-            at = block * channels + field * levels
-            rhs_ref[at : at + levels, :] = jnp.where(inside, advanced[field], 0.0).astype(
-                jnp.bfloat16
-            )
-    partial = jnp.dot(rhs_ref[...], near_ref[...], preferred_element_type=jnp.float32)
-    real = jnp.zeros((channels, lane_count), jnp.float32)
-    imag = jnp.zeros((channels, lane_count), jnp.float32)
-    for block in range(blocks):
-        part_real = partial[block * channels : (block + 1) * channels, :lane_count]
-        part_imag = partial[block * channels : (block + 1) * channels, lane_count:]
-        far_real = far_ref[block : block + 1, :lane_count]
-        far_imag = far_ref[block : block + 1, lane_count:]
-        real = real + (part_real * far_real - part_imag * far_imag)
-        imag = imag + (part_real * far_imag + part_imag * far_real)
+            for block in range(blocks):
+                at = (field * blocks + block) * piece_rows
+                part_real = partial[at : at + piece_rows, :lane_count]
+                part_imag = partial[at : at + piece_rows, lane_count:]
+                far_real = far_ref[block : block + 1, :lane_count]
+                far_imag = far_ref[block : block + 1, lane_count:]
+                add_real = part_real * far_real - part_imag * far_imag
+                add_imag = part_real * far_imag + part_imag * far_real
+                total = field * chunks + chunk
+                real[total] = add_real if block == 0 else real[total] + add_real
+                imag[total] = add_imag if block == 0 else imag[total] + add_imag
     scale = jnp.full((1, lane_count), weights_ref[0], jnp.float32) / points_row
     half_rows = 2 * per_part
-    for phase, value in enumerate((real, imag)):
-        turned = jnp.pad(value * scale, ((0, lane_count - channels), (0, 0))).T
+    rest = jnp.zeros((lane_count - channels, lane_count), jnp.float32)
+    for phase, values in enumerate((real, imag)):
+        turned = jnp.concatenate([value * scale for value in values] + [rest], axis=0).T
         for at in range(half_rows):
             wave_ref[pl.ds(phase * half_rows + at, sources, stride=piece_rows), :] = turned[
                 at * sources : (at + 1) * sources
             ]
 
-    copies[2].wait()
+    copies[1 + chunks].wait()
     slot_total = highest + 1
     left = lane_count - channels
     for part in range(active):
@@ -299,24 +329,62 @@
         sent_ref[at] = jnp.zeros((2 * piece_rows, lane_count), jnp.bfloat16)
 
 
-def spectral_kernel(
+def prepare_kernel(
     dims,
-    received_ref,
-    position_ref,
+    part_ref,
+    group_ref,
+    points_ref,
+    table_ref,
     pairs_ref,
     depths_ref,
     diffusion_ref,
-    sent_ref,
-    wave_ref,
+    near_ref,
+    far_ref,
+    solve_ref,
+    rows_ref,
 ):
+    levels, lon_count, group_count, slot_count, parts, per_part, highest = dims
+    points_row = jnp.full((1, lane_count), points_ref[0], jnp.int32).astype(jnp.float32)
+    wave = wave_row(dims, table_ref[...])
+    near_ref[...] = factors(lane_count, 1, wave, points_row).astype(jnp.bfloat16)
+    far_ref[...] = factors(far_ref.shape[0], lane_count, wave, points_row)
+
+    part, group = part_ref[0], group_ref[0]
+    lane_row = lax.broadcasted_iota(jnp.int32, (1, lane_count), 1)
+    depth_row = jnp.zeros((1, lane_count), jnp.float32)
+    damp_row = jnp.zeros((1, lane_count), jnp.float32)
+    for level in range(levels):
+        depth_row = jnp.where(lane_row % levels == level, depths_ref[level], depth_row)
+        damp_row = jnp.where(lane_row == level, diffusion_ref[level], damp_row)
+    is_first = lane_row < levels
+    coeff_row = jnp.where(is_first, damp_row, depth_row)
+    rows_ref[0:1, :] = depth_row
+    position = lax.broadcasted_iota(jnp.int32, (lane_count, lane_count), 0)
+    for index in range(per_part):
+        pair = pairs_ref[group, jnp.minimum(part * per_part + index, slot_count - 1)]
+        lower_half = position < highest - pair
+        total = jnp.where(lower_half, pair + position, position - 1).astype(jnp.float32)
+        operator = total * (total + 1.0) / float(highest * highest)
+        factor = jnp.where(is_first, operator * operator, operator)
+        solve_ref[3 * index] = 1.0 + coeff_row * factor
+        solve_ref[3 * index + 1] = jnp.where(is_first, 0.0, operator)
+        solve_ref[3 * index + 2] = jnp.where(lower_half, 1.0, 0.0)
+        for half in range(2):
+            wavenumber = pair if half == 0 else highest - 1 - pair
+            at = 1 + half * per_part + index
+            rows_ref[at : at + 1, :] = jnp.full(
+                (1, lane_count), jnp.where(wavenumber == 0, 1.0, 2.0), jnp.float32
+            )
+
+
+def spectral_kernel(dims, received_ref, group_ref, solve_ref, rows_ref, sent_ref, wave_ref):
     levels, lon_count, group_count, slot_count, parts, per_part, highest = dims
     channels = 3 * levels
     slot_total = highest + 1
     left = lane_count - channels
     sources = parts * group_count
-    part, group = position_ref[0], position_ref[1]
-    tile = (piece_rows, lane_count)
-    lane = lax.broadcasted_iota(jnp.int32, tile, 1)
+    group = group_ref[0]
+    lane = lax.broadcasted_iota(jnp.int32, (piece_rows, lane_count), 1)
     for source in range(sources):
         wave_ref[source * piece_rows : (source + 1) * piece_rows, :] = received_ref[
             source, :piece_rows, :
@@ -329,58 +397,52 @@
         rest = pltpu.roll(lower, (lane_count - (slot_total - left)) % lane_count, 1)
         first.append(jnp.where(lane < left, start, jnp.where(lane < slot_total, rest, 0.0)))
         second.append(jnp.where(lane < slot_total, lower, 0.0))
-    bases = [
-        jnp.concatenate(first, axis=0).astype(jnp.bfloat16),
-        jnp.concatenate(second, axis=0).astype(jnp.bfloat16),
-    ]
-    row_tile = (1, lane_count)
-    lane_row = lax.broadcasted_iota(jnp.int32, row_tile, 1)
-    depth_row = jnp.zeros(row_tile, jnp.float32)
-    damp_row = jnp.zeros(row_tile, jnp.float32)
-    for level in range(levels):
-        depth_row = jnp.where(lane_row % levels == level, depths_ref[level], depth_row)
-        damp_row = jnp.where(lane_row == level, diffusion_ref[level], damp_row)
-    is_first = lane_row < levels
+    bases = [jnp.concatenate(first, axis=0), jnp.concatenate(second, axis=0)]
+    lane_row = lax.broadcasted_iota(jnp.int32, (1, lane_count), 1)
     is_last = lane_row >= 2 * levels
-    coeff_row = jnp.where(is_first, damp_row, depth_row)
-    column_tile = (lane_count, 1)
-    position = lax.broadcasted_iota(jnp.int32, column_tile, 0)
+    depth_row = rows_ref[0:1, :]
     for index in range(per_part):
-        pair = pairs_ref[group, jnp.minimum(part * per_part + index, slot_count - 1)]
-        lower_half = position < highest - pair
-        total = jnp.where(lower_half, pair + position, position - 1).astype(jnp.float32)
-        operator = total * (total + 1.0) / float(highest * highest)
-        factor = jnp.where(is_first, operator * operator, operator)
-        divisor = 1.0 + coeff_row * factor
-        basis = bases[index]
-        basis_turned = basis.astype(jnp.float32).T.astype(jnp.bfloat16)
+        basis = bases[index].astype(jnp.bfloat16)
+        basis_turned = bases[index].T.astype(jnp.bfloat16)
+        specs = []
+        for half in range(2):
+            waves = jnp.concatenate(
+                [
+                    wave_ref[
+                        pl.ds((phase * 2 + half) * per_part + index, sources, stride=piece_rows), :
+                    ]
+                    for phase in range(2)
+                ],
+                axis=1,
+            ).astype(jnp.bfloat16)
+            specs.append(jnp.dot(basis_turned, waves, preferred_element_type=jnp.float32))
+        lower_half = solve_ref[3 * index + 2] > 0.5
         solved = []
         for phase in range(2):
-            halves = []
-            for half in range(2):
-                at = (phase * 2 + half) * per_part + index
-                waves = wave_ref[pl.ds(at, sources, stride=piece_rows), :].astype(jnp.bfloat16)
-                halves.append(
-                    jnp.dot(basis_turned, waves, preferred_element_type=jnp.float32)
-                )
-            spec = jnp.where(lower_half, halves[0], halves[1])
+            lanes = slice(phase * lane_count, (phase + 1) * lane_count)
+            spec = jnp.where(lower_half, specs[0][:, lanes], specs[1][:, lanes])
             thermal = pltpu.roll(spec, lane_count - levels, 1)
-            top = jnp.where(is_first, spec, spec + operator * thermal)
-            quotient = top / divisor
+            quotient = (spec + solve_ref[3 * index + 1] * thermal) / solve_ref[3 * index]
             moved = pltpu.roll(quotient, levels, 1)
             solved.append(jnp.where(is_last, spec - depth_row * moved, quotient))
-        for phase in range(2):
-            for half in range(2):
+        for half in range(2):
+            kept = jnp.concatenate(
+                [
+                    jnp.where(lower_half, value, 0.0)
+                    if half == 0
+                    else jnp.where(lower_half, 0.0, value)
+                    for value in solved
+                ],
+                axis=1,
+            ).astype(jnp.bfloat16)
+            back = jnp.dot(basis, kept, preferred_element_type=jnp.float32)
+            row = 1 + half * per_part + index
+            doubling = rows_ref[row : row + 1, :]
+            for phase in range(2):
                 at = (phase * 2 + half) * per_part + index
-                kept = jnp.where(
-                    lower_half if half == 0 else jnp.logical_not(lower_half), solved[phase], 0.0
+                wave_ref[pl.ds(at, sources, stride=piece_rows), :] = (
+                    back[:, phase * lane_count : (phase + 1) * lane_count] * doubling
                 )
-                back = jnp.dot(
-                    basis, kept.astype(jnp.bfloat16), preferred_element_type=jnp.float32
-                )
-                wavenumber = pair if half == 0 else highest - 1 - pair
-                doubling = jnp.where(wavenumber == 0, 1.0, 2.0)
-                wave_ref[pl.ds(at, sources, stride=piece_rows), :] = back * doubling
     for source in range(sources):
         sent_ref[source] = wave_ref[
             source * piece_rows : (source + 1) * piece_rows, :
@@ -388,13 +450,25 @@
 
 
 def synthesis_kernel(
-    dims, received_ref, near_ref, far_ref, points_ref, out_ref, wave_ref, rotated_ref
+    dims,
+    received_ref,
+    near_ref,
+    far_ref,
+    points_ref,
+    out_hbm,
+    wave_ref,
+    rotated_ref,
+    out_ref,
+    sems,
 ):
     levels, lon_count, group_count, slot_count, parts, per_part, highest = dims
-    channels = 3 * levels
     blocks = lon_count // lane_count
     sources = parts * group_count
     half_rows = 2 * per_part
+    level_rows = 3 * blocks
+    chunks = levels // piece_rows
+    chunk_rows = piece_rows * level_rows
+    padded = (level_rows + level_rows % 2) * piece_rows
     for source in range(sources):
         wave_ref[source * piece_rows : (source + 1) * piece_rows, :] = received_ref[source].astype(
             jnp.float32
@@ -406,30 +480,48 @@
                 for at in range(half_rows)
             ],
             axis=0,
-        ).T[:channels]
+        ).T
         for phase in range(2)
     )
-    for block in range(blocks):
-        far_real = far_ref[block : block + 1, :lane_count]
-        far_imag = far_ref[block : block + 1, lane_count:]
-        rotated_ref[block * channels : (block + 1) * channels, :] = jnp.concatenate(
-            [real * far_real + imag * far_imag, imag * far_real - real * far_imag], axis=1
-        ).astype(jnp.bfloat16)
-    result = lax.dot_general(
-        rotated_ref[...],
-        near_ref[...],
-        (((1,), (1,)), ((), ())),
-        preferred_element_type=jnp.float32,
-    )
-    lane_wide = lax.broadcasted_iota(jnp.int32, (levels, lane_count), 1)
     points = points_ref[0]
-    for block in range(blocks):
-        inside = lane_wide + block * lane_count < points
+    lane = lax.broadcasted_iota(jnp.int32, (piece_rows, lane_count), 1)
+    copies = []
+    for chunk in range(chunks):
+        units = []
         for field in range(3):
-            at = block * channels + field * levels
-            out_ref[pl.ds(field * blocks + block, levels, stride=3 * blocks), :] = jnp.where(
-                inside, result[at : at + levels], 0.0
+            at = field * levels + chunk * piece_rows
+            part_real, part_imag = real[at : at + piece_rows], imag[at : at + piece_rows]
+            for block in range(blocks):
+                far_real = far_ref[block : block + 1, :lane_count]
+                far_imag = far_ref[block : block + 1, lane_count:]
+                units.append(
+                    jnp.concatenate(
+                        [
+                            part_real * far_real + part_imag * far_imag,
+                            part_imag * far_real - part_real * far_imag,
+                        ],
+                        axis=1,
+                    )
+                )
+        for at, two in enumerate(pair_rows(units)):
+            start = chunk * padded + at * 2 * piece_rows
+            rotated_ref[start : start + 2 * piece_rows, :] = two.astype(jnp.bfloat16)
+        result = lax.dot_general(
+            rotated_ref[chunk * padded : (chunk + 1) * padded, :],
+            near_ref[...],
+            (((1,), (1,)), ((), ())),
+            preferred_element_type=jnp.float32,
+        )
+        for unit in range(level_rows):
+            inside = lane < points - unit % blocks * lane_count
+            out_ref[pl.ds(chunk * chunk_rows + unit, piece_rows, stride=level_rows), :] = (
+                jnp.where(inside, result[unit * piece_rows : (unit + 1) * piece_rows], 0.0)
             )
+        rows = pl.ds(chunk * chunk_rows, chunk_rows)
+        copies.append(pltpu.make_async_copy(out_ref.at[rows], out_hbm.at[rows], sems.at[chunk]))
+        copies[-1].start()
+    for copy in copies:
+        copy.wait()
 
 
 def packed_body(
@@ -448,53 +540,72 @@
     blocks = lon_count // lane_count
     sources = parts * group_count
     far_rows = -(-blocks // piece_rows) * piece_rows
+    chunks = levels // piece_rows
+    padded = (3 * blocks + 3 * blocks % 2) * piece_rows * chunks
     in_vmem = pl.BlockSpec(memory_space=pltpu.VMEM)
     in_smem = pl.BlockSpec(memory_space=pltpu.SMEM)
     in_hbm = pl.BlockSpec(memory_space=pltpu.HBM)
     params = pltpu.CompilerParams(vmem_limit_bytes=16 << 20)
     grid = prognostic_arrays.reshape(channels * blocks, lane_count)
-    position = jnp.stack([lax.axis_index("lat"), lax.axis_index("lev")]).astype(jnp.int32)
     basis = jnp.swapaxes(legendre, 2, 3)
-    sent, near, far = pl.pallas_call(
+    part = lax.axis_index("lat").astype(jnp.int32).reshape(1)
+    group = lax.axis_index("lev").astype(jnp.int32).reshape(1)
+    sent = pl.pallas_call(
         functools.partial(analysis_kernel, dims),
         name="analysis",
-        out_shape=(
-            jax.ShapeDtypeStruct((sources, 2 * piece_rows, lane_count), jnp.bfloat16),
-            jax.ShapeDtypeStruct((lane_count, 2 * lane_count), jnp.bfloat16),
-            jax.ShapeDtypeStruct((far_rows, 2 * lane_count), jnp.float32),
-        ),
+        out_shape=jax.ShapeDtypeStruct((sources, 2 * piece_rows, lane_count), jnp.bfloat16),
         in_specs=[in_hbm, in_smem, in_smem, in_smem, in_hbm, in_hbm],
-        out_specs=(in_vmem, in_vmem, in_vmem),
+        out_specs=in_vmem,
         scratch_shapes=[
             pltpu.VMEM(grid.shape, jnp.float32),
             pltpu.VMEM(owner_pairs.shape, jnp.int32),
             pltpu.VMEM(basis.shape, jnp.bfloat16),
-            pltpu.VMEM((blocks * channels, lane_count), jnp.bfloat16),
+            pltpu.VMEM((lane_count, 2 * lane_count), jnp.bfloat16),
+            pltpu.VMEM((far_rows, 2 * lane_count), jnp.float32),
+            pltpu.VMEM((padded, lane_count), jnp.bfloat16),
             pltpu.VMEM((sources * piece_rows, lane_count), jnp.float32),
-            pltpu.SemaphoreType.DMA((3,)),
+            pltpu.SemaphoreType.DMA((2 + chunks,)),
         ],
         compiler_params=pltpu.CompilerParams(vmem_limit_bytes=67043328),
     )(grid, coriolis, weights, row_points, owner_pairs, basis)
     received = lax.all_to_all(sent, ("lat", "lev"), split_axis=0, concat_axis=0, tiled=True)
+    near, far, solve, rows = pl.pallas_call(
+        functools.partial(prepare_kernel, dims),
+        name="prepare",
+        out_shape=(
+            jax.ShapeDtypeStruct((lane_count, 2 * lane_count), jnp.bfloat16),
+            jax.ShapeDtypeStruct((far_rows, 2 * lane_count), jnp.float32),
+            jax.ShapeDtypeStruct((3 * per_part, lane_count, lane_count), jnp.float32),
+            jax.ShapeDtypeStruct((piece_rows, lane_count), jnp.float32),
+        ),
+        in_specs=[in_smem, in_smem, in_smem, in_vmem, in_smem, in_smem, in_smem],
+        out_specs=(in_vmem,) * 4,
+        compiler_params=params,
+        cost_estimate=pl.CostEstimate(
+            flops=40 * lane_count * lane_count, bytes_accessed=1 << 19, transcendentals=0
+        ),
+    )(part, group, row_points, owner_pairs, owner_pairs, depths, diffusion)
     solved = pl.pallas_call(
         functools.partial(spectral_kernel, dims),
         name="spectral",
         out_shape=jax.ShapeDtypeStruct((sources, piece_rows, lane_count), jnp.bfloat16),
-        in_specs=[in_vmem, in_smem, in_smem, in_smem, in_smem],
+        in_specs=[in_vmem, in_smem, in_vmem, in_vmem],
         out_specs=in_vmem,
         scratch_shapes=[pltpu.VMEM((sources * piece_rows, lane_count), jnp.float32)],
         compiler_params=params,
-    )(received, position, owner_pairs, depths, diffusion)
+    )(received, group, solve, rows)
     returned = lax.all_to_all(solved, ("lat", "lev"), split_axis=0, concat_axis=0, tiled=True)
     updated = pl.pallas_call(
         functools.partial(synthesis_kernel, dims),
         name="synthesis",
         out_shape=jax.ShapeDtypeStruct((channels * blocks, lane_count), jnp.float32),
         in_specs=[in_vmem, in_vmem, in_vmem, in_smem],
-        out_specs=in_vmem,
+        out_specs=in_hbm,
         scratch_shapes=[
             pltpu.VMEM((sources * piece_rows, lane_count), jnp.float32),
-            pltpu.VMEM((blocks * channels, 2 * lane_count), jnp.bfloat16),
+            pltpu.VMEM((padded, 2 * lane_count), jnp.bfloat16),
+            pltpu.VMEM((channels * blocks, lane_count), jnp.float32),
+            pltpu.SemaphoreType.DMA((chunks,)),
         ],
         compiler_params=params,
     )(returned, near, far, row_points)

time: 31.8 us -> 31.4 us (0.987)
  waiting for transfers between devices: 7.69 us -> 6.18 us
  local copies, waits for them, and re-layouts: 0.03 us -> 0.67 us
  Pallas kernels: 4.99 us -> 5.42 us
    all_to_all x1, waiting for transfers between devices: 7.69 us -> 6.18 us  [packed_body(): lax.all_to_all(sent, ('lat', 'lev'), split_axis=0, concat_axis=0, tiled=T...]
    pallas_call x0 -> x1, Pallas kernels: none -> 0.92 us  [packed_body(): pl.pallas_call(functools.partial(prepare_kernel, dims), name='prepare', o...]
    unnamed x10 -> x6, local copies, waits for them, and re-layouts: 0.03 us -> 0.67 us
    pallas_call x1, Pallas kernels: 1.58 us -> 0.96 us  [packed_body(): pl.pallas_call(functools.partial(spectral_kernel, dims), name='spectral',...]
  transfers between devices with their start and end apart: 1 -> 1, of which waited for: 1 -> 1; matrix products, arithmetic and copies ran while one was open for 0% -> 0% of each run, Pallas kernels for 0% -> 3%
where the time goes in v5:
time: 31.4 us; the launch traced here: 31 us
  blocking collectives  9.44 us (30%)
  starting transfers between devices  7.33 us (23%)
  waiting for transfers between devices  6.18 us (20%)
  Pallas kernels  5.42 us (17%)
  between operations  2 us (6%)
  local copies, waits for them, and re-layouts  0.67 us (2%)
    all_to_all x1, blocking collectives, packed_body(): lax.all_to_all(solved, ('lat', 'lev'), split_axis=0, concat_axis=0, tiled...  9.44 us
    all_to_all x1, starting transfers between devices, packed_body(): lax.all_to_all(sent, ('lat', 'lev'), split_axis=0, concat_axis=0, tiled=T...  7.33 us
    all_to_all x1, waiting for transfers between devices, packed_body(): lax.all_to_all(sent, ('lat', 'lev'), split_axis=0, concat_axis=0, tiled=T...  6.18 us
    pallas_call x1, Pallas kernels, packed_body(): pl.pallas_call(functools.partial(analysis_kernel, dims), name='analysis',...  2.38 us
    pallas_call x1, Pallas kernels, packed_body(): pl.pallas_call(functools.partial(synthesis_kernel, dims), name='synthesis...  1.16 us
    pallas_call x1, Pallas kernels, packed_body(): pl.pallas_call(functools.partial(spectral_kernel, dims), name='spectral',...  0.96 us
    pallas_call x1, Pallas kernels, packed_body(): pl.pallas_call(functools.partial(prepare_kernel, dims), name='prepare', o...  0.92 us
    unnamed x6, local copies, waits for them, and re-layouts  0.67 us
  transfers between devices with their start and end apart: 1, of which 1 were waited for; matrix products, arithmetic and copies ran while one was open for 0% of the time, Pallas kernels for 3%

profile of v5, /device:TPU:0, one launch (start us, length us, event | category | flops | bytes accessed | tf_op | source)
XLA Modules:
  0.0 31.0 jit_solution(6338310982457950756)
XLA Ops:
  1.9 2.4 %analysis.1 = bf16[32,16,128]{2,1,0:T(8,128)(2,1)} custom-call(f32[1008,128]{1,0:T(8,128)} %bitcast.5, f32[1]{0:T(128)S(6)} %copy.11.coriolis_ref, f32[1]{0:T(128)S(6)} %copy.12.weights_ref, s32[1]{0:T(128)S(6)} %copy.13.points_ref, s32[8,6]{1,0:T(8,128)} %pairs_ref.1, bf16[1,6,8,97]{3,2,1,0:T(8,128)(2,1)} %bitcast.6), custom_call_target="tpu_custom_call" | custom-call | tf_op jit(solution)/shard_map/analysis/pallas_call | solution.py:553
  4.3 7.3 %all-to-all-start = ((bf16[32,16,128]{2,1,0:T(8,128)(2,1)}), bf16[32,16,128]{2,1,0:T(8,128)(2,1)S(1)}, u32[]{:S(2)}, u32[]{:S(2)}) async-start(bf16[32,16,128]{2,1,0:T(8,128)(2,1)} %analysis.1), calls=%async_computation | async-start | bytes 262144 | tf_op jit(solution)/shard_map/all_to_all | solution.py:571
  11.7 0.0 copy-start
  11.7 0.0 copy-start.1
  11.7 0.0 copy-start.2
  11.7 0.7 %copy-done = s32[8,6]{1,0:T(8,128)S(1)} copy-done((s32[8,6]{1,0:T(8,128)S(1)}, s32[8,6]{1,0:T(8,128)}, u32[]{:S(2)}) %copy-start) | copy-done | bytes 216
  12.4 0.0 copy-done.1
  12.4 0.0 copy-done.2
  12.4 0.9 %prepare.1 = (bf16[128,256]{1,0:T(8,128)(2,1)S(1)}, f32[24,256]{1,0:T(8,128)S(1)}, f32[6,128,128]{2,1,0:T(8,128)S(1)}, f32[8,128]{1,0:T(8,128)S(1)}) custom-call(s32[1]{0:T(128)} %bitcast.3.part_ref, s32[1]{0:T(128)} %bitcast.2.group_ref, s32[1]{0:T(128)S(6)} %copy.13.points_ref, s32[8,6]{1,0:T(8,128)S(1)} %copy-done, s32[8,6]{1,0:T(8,128)S(1)} %copy-done, ...), custom_call_target="tpu_custom_call" | custom-call | flops 655360 | bytes 524288 | tf_op jit(solution)/shard_map/prepare/pallas_call | solution.py:572
  13.3 6.2 %all-to-all-done.received_ref = bf16[32,16,128]{2,1,0:T(8,128)(2,1)S(1)} async-done(((bf16[32,16,128]{2,1,0:T(8,128)(2,1)}), bf16[32,16,128]{2,1,0:T(8,128)(2,1)S(1)}, u32[]{:S(2)}, u32[]{:S(2)}) %all-to-all-start) | async-done | bytes 131104 | tf_op jit(solution)/shard_map/all_to_all | solution.py:571
  19.5 1.0 %spectral.1 = bf16[32,8,128]{2,1,0:T(8,128)(2,1)S(1)} custom-call(bf16[32,16,128]{2,1,0:T(8,128)(2,1)S(1)} %all-to-all-done.received_ref, s32[1]{0:T(128)} %bitcast.2.group_ref, f32[6,128,128]{2,1,0:T(8,128)S(1)} %get-tuple-element.9.solve_ref, f32[8,128]{1,0:T(8,128)S(1)} %get-tuple-element.10.rows_ref), custom_call_target="tpu_custom_call" | custom-call | tf_op jit(solution)/shard_map/spectral/pallas_call | solution.py:588
  20.4 9.4 %all_to_all.10.received_ref = bf16[32,8,128]{2,1,0:T(8,128)(2,1)S(1)} all-to-all(bf16[32,8,128]{2,1,0:T(8,128)(2,1)S(1)} %spectral.1), channel_id=1, replica_groups=mesh['lat'=4,'lev'=8] {'lat','lev'}, dimensions={0} | all-to-all | bytes 131072 | tf_op jit(solution)/shard_map/all_to_all | solution.py:597
  29.9 1.2 %synthesis.1 = f32[1008,128]{1,0:T(8,128)} custom-call(bf16[32,8,128]{2,1,0:T(8,128)(2,1)S(1)} %all_to_all.10.received_ref, bf16[128,256]{1,0:T(8,128)(2,1)S(1)} %get-tuple-element.11.near_ref, f32[24,256]{1,0:T(8,128)S(1)} %get-tuple-element.12.far_ref, s32[1]{0:T(128)S(6)} %copy.13.points_ref), custom_call_target="tpu_custom_call" | custom-call | tf_op jit(solution)/shard_map/synthesis/pallas_call | solution.py:598
Async XLA Ops:
  4.3 15.1 %all-to-all-start = ((bf16[32,16,128]{2,1,0:T(8,128)(2,1)}), bf16[32,16,128]{2,1,0:T(8,128)(2,1)S(1)}, u32[]{:S(2)}, u32[]{:S(2)}) async-start(bf16[32,16,128]{2,1,0:T(8,128)(2,1)} %analysis.1), calls=%async_computation | async-start | bytes 262144 | tf_op jit(solution)/shard_map/all_to_all | solution.py:571
  11.7 0.7 %copy-start = (s32[8,6]{1,0:T(8,128)S(1)}, s32[8,6]{1,0:T(8,128)}, u32[]{:S(2)}) copy-start(s32[8,6]{1,0:T(8,128)} %pairs_ref.1) | copy-start | bytes 580
  11.7 0.7 %copy-start.1 = (f32[16]{0:T(128)S(1)}, f32[16]{0:T(128)}, u32[]{:S(2)}) copy-start(f32[16]{0:T(128)} %depths_ref.1) | copy-start | bytes 196
  11.7 0.7 %copy-start.2 = (f32[16]{0:T(128)S(1)}, f32[16]{0:T(128)}, u32[]{:S(2)}) copy-start(f32[16]{0:T(128)} %diffusion_ref.1) | copy-start | bytes 196

commit v6 on v5

--- a/solution.py
+++ b/solution.py
@@ -177,8 +177,9 @@
     tile = (piece_rows, lane_count)
     row = lax.broadcasted_iota(jnp.int32, tile, 0)
     lane = lax.broadcasted_iota(jnp.int32, tile, 1)
-    lane_slot = lane // group_count % parts * per_part + lane // sources % per_part
-    at_group = lane % group_count == row
+    lane_part = (lane >> (group_count.bit_length() - 1)) & (parts - 1)
+    lane_slot = lane_part * per_part + ((lane >> (sources.bit_length() - 1)) & (per_part - 1))
+    at_group = (lane & (group_count - 1)) == row
     spread = jnp.zeros(tile, jnp.float32)
     for slot in range(slot_count):
         chosen = jnp.logical_and(at_group, lane_slot == slot)
@@ -193,13 +194,32 @@
     cosine, sine = turn_cos_sin(
         turns_of(place.astype(jnp.float32) * wave, points_row, 1.0 / points_row)
     )
-    return jnp.concatenate([cosine, -sine], axis=1)
-
-
-def pair_rows(units):
-    if len(units) % 2:
-        units = units + [jnp.zeros_like(units[0])]
-    return [jnp.concatenate(units[at : at + 2], axis=0) for at in range(0, len(units), 2)]
+    return cosine, -sine
+
+
+def fill_factors(wave, points_row, near_ref, far_ref, step_ref):
+    span = near_ref.shape[0]
+    base_real, base_imag = factors(piece_rows, 1, wave, points_row)
+    step_real, step_imag = factors(span // piece_rows, piece_rows, wave, points_row)
+    step_ref[:, :lane_count] = step_real
+    step_ref[:, lane_count:] = step_imag
+    for at in range(0, span // piece_rows, 2):
+        rows = []
+        for index in (at, at + 1):
+            real = step_ref[index : index + 1, :lane_count]
+            imag = step_ref[index : index + 1, lane_count:]
+            rows.append(
+                jnp.concatenate(
+                    [base_real * real - base_imag * imag, base_real * imag + base_imag * real],
+                    axis=1,
+                )
+            )
+        near_ref[at * piece_rows : (at + 2) * piece_rows, :] = jnp.concatenate(
+            rows, axis=0
+        ).astype(jnp.bfloat16)
+    far_real, far_imag = factors(far_ref.shape[0], span, wave, points_row)
+    far_ref[:, :lane_count] = far_real
+    far_ref[:, lane_count:] = far_imag
 
 
 def analysis_kernel(
@@ -216,6 +236,7 @@
     legendre_ref,
     near_ref,
     far_ref,
+    step_ref,
     rhs_ref,
     wave_ref,
     sems,
@@ -242,61 +263,48 @@
     points = points_ref[0]
     points_row = jnp.full((1, lane_count), points, jnp.int32).astype(jnp.float32)
     wave = wave_row(dims, pairs_ref[...])
-    near_ref[...] = factors(lane_count, 1, wave, points_row).astype(jnp.bfloat16)
-    far_ref[...] = factors(far_ref.shape[0], lane_count, wave, points_row)
+    fill_factors(wave, points_row, near_ref, far_ref, step_ref)
+    tiles = near_ref.shape[0] // lane_count
     rotation = coriolis_ref[0]
-    tile = (piece_rows, lane_count)
-    lane = lax.broadcasted_iota(jnp.int32, tile, 1)
-    padded = (level_rows + level_rows % 2) * piece_rows
-    real = [None] * (3 * chunks)
-    imag = [None] * (3 * chunks)
+    half_rotation = stepsize_delta * rotation
+    lane = lax.broadcasted_iota(jnp.int32, (piece_rows, lane_count), 1)
+    lane_wide = lax.broadcasted_iota(jnp.int32, (levels, lane_count), 1)
     for chunk in range(chunks):
         copies[1 + chunk].wait()
-        units = []
+    for block in range(blocks):
+        vorticity, spreading, thermal = (
+            grid_ref[pl.ds(field * blocks + block, levels, stride=level_rows), :]
+            for field in range(3)
+        )
+        inside = lane_wide < points - block * lane_count
+        stepped = stepsize_delta * spreading
+        advanced = (
+            vorticity - (rotation + vorticity) * stepped,
+            spreading + (half_rotation * vorticity - spreading * stepped),
+            thermal - thermal * stepped,
+        )
+        lanes = slice(block % tiles * lane_count, (block % tiles + 1) * lane_count)
         for field in range(3):
-            for block in range(blocks):
-
-                def load(which):
-                    at = chunk * chunk_rows + which * blocks + block
-                    return grid_ref[pl.ds(at, piece_rows, stride=level_rows), :]
-
-                spreading = load(1)
-                if field == 0:
-                    vorticity = load(0)
-                    value = vorticity - stepsize_delta * (rotation + vorticity) * spreading
-                elif field == 1:
-                    value = spreading + stepsize_delta * (
-                        rotation * load(0) - spreading * spreading
-                    )
-                else:
-                    thermal = load(2)
-                    value = thermal - stepsize_delta * thermal * spreading
-                units.append(jnp.where(lane < points - block * lane_count, value, 0.0))
-        for at, two in enumerate(pair_rows(units)):
-            start = chunk * padded + at * 2 * piece_rows
-            rhs_ref[start : start + 2 * piece_rows, :] = two.astype(jnp.bfloat16)
-        partial = jnp.dot(
-            rhs_ref[chunk * padded : (chunk + 1) * padded, :],
-            near_ref[...],
-            preferred_element_type=jnp.float32,
-        )
-        for field in range(3):
-            for block in range(blocks):
-                at = (field * blocks + block) * piece_rows
-                part_real = partial[at : at + piece_rows, :lane_count]
-                part_imag = partial[at : at + piece_rows, lane_count:]
-                far_real = far_ref[block : block + 1, :lane_count]
-                far_imag = far_ref[block : block + 1, lane_count:]
-                add_real = part_real * far_real - part_imag * far_imag
-                add_imag = part_real * far_imag + part_imag * far_real
-                total = field * chunks + chunk
-                real[total] = add_real if block == 0 else real[total] + add_real
-                imag[total] = add_imag if block == 0 else imag[total] + add_imag
+            at = block // tiles * channels + field * levels
+            rhs_ref[at : at + levels, lanes] = jnp.where(inside, advanced[field], 0.0).astype(
+                jnp.bfloat16
+            )
+    partial = jnp.dot(rhs_ref[...], near_ref[...], preferred_element_type=jnp.float32)
+    real, imag = None, None
+    for block in range(blocks // tiles):
+        part_real = partial[block * channels : (block + 1) * channels, :lane_count]
+        part_imag = partial[block * channels : (block + 1) * channels, lane_count:]
+        far_real = far_ref[block : block + 1, :lane_count]
+        far_imag = far_ref[block : block + 1, lane_count:]
+        add_real = part_real * far_real - part_imag * far_imag
+        add_imag = part_real * far_imag + part_imag * far_real
+        real = add_real if block == 0 else real + add_real
+        imag = add_imag if block == 0 else imag + add_imag
     scale = jnp.full((1, lane_count), weights_ref[0], jnp.float32) / points_row
     half_rows = 2 * per_part
     rest = jnp.zeros((lane_count - channels, lane_count), jnp.float32)
-    for phase, values in enumerate((real, imag)):
-        turned = jnp.concatenate([value * scale for value in values] + [rest], axis=0).T
+    for phase, value in enumerate((real, imag)):
+        turned = jnp.concatenate([value * scale, rest], axis=0).T
         for at in range(half_rows):
             wave_ref[pl.ds(phase * half_rows + at, sources, stride=piece_rows), :] = turned[
                 at * sources : (at + 1) * sources
@@ -342,12 +350,12 @@
     far_ref,
     solve_ref,
     rows_ref,
+    step_ref,
 ):
     levels, lon_count, group_count, slot_count, parts, per_part, highest = dims
     points_row = jnp.full((1, lane_count), points_ref[0], jnp.int32).astype(jnp.float32)
     wave = wave_row(dims, table_ref[...])
-    near_ref[...] = factors(lane_count, 1, wave, points_row).astype(jnp.bfloat16)
-    far_ref[...] = factors(far_ref.shape[0], lane_count, wave, points_row)
+    fill_factors(wave, points_row, near_ref, far_ref, step_ref)
 
     part, group = part_ref[0], group_ref[0]
     lane_row = lax.broadcasted_iota(jnp.int32, (1, lane_count), 1)
@@ -359,14 +367,14 @@
     is_first = lane_row < levels
     coeff_row = jnp.where(is_first, damp_row, depth_row)
     rows_ref[0:1, :] = depth_row
-    position = lax.broadcasted_iota(jnp.int32, (lane_count, lane_count), 0)
+    position = lax.broadcasted_iota(jnp.int32, (solve_ref.shape[1], lane_count), 0)
     for index in range(per_part):
         pair = pairs_ref[group, jnp.minimum(part * per_part + index, slot_count - 1)]
         lower_half = position < highest - pair
         total = jnp.where(lower_half, pair + position, position - 1).astype(jnp.float32)
         operator = total * (total + 1.0) / float(highest * highest)
         factor = jnp.where(is_first, operator * operator, operator)
-        solve_ref[3 * index] = 1.0 + coeff_row * factor
+        solve_ref[3 * index] = 1.0 / (1.0 + coeff_row * factor)
         solve_ref[3 * index + 1] = jnp.where(is_first, 0.0, operator)
         solve_ref[3 * index + 2] = jnp.where(lower_half, 1.0, 0.0)
         for half in range(2):
@@ -401,9 +409,10 @@
     lane_row = lax.broadcasted_iota(jnp.int32, (1, lane_count), 1)
     is_last = lane_row >= 2 * levels
     depth_row = rows_ref[0:1, :]
+    held = solve_ref.shape[1]
     for index in range(per_part):
-        basis = bases[index].astype(jnp.bfloat16)
-        basis_turned = bases[index].T.astype(jnp.bfloat16)
+        basis = bases[index].astype(jnp.bfloat16)[:, :held]
+        basis_turned = bases[index].T[:held].astype(jnp.bfloat16)
         specs = []
         for half in range(2):
             waves = jnp.concatenate(
@@ -422,7 +431,7 @@
             lanes = slice(phase * lane_count, (phase + 1) * lane_count)
             spec = jnp.where(lower_half, specs[0][:, lanes], specs[1][:, lanes])
             thermal = pltpu.roll(spec, lane_count - levels, 1)
-            quotient = (spec + solve_ref[3 * index + 1] * thermal) / solve_ref[3 * index]
+            quotient = (spec + solve_ref[3 * index + 1] * thermal) * solve_ref[3 * index]
             moved = pltpu.roll(quotient, levels, 1)
             solved.append(jnp.where(is_last, spec - depth_row * moved, quotient))
         for half in range(2):
@@ -462,13 +471,13 @@
     sems,
 ):
     levels, lon_count, group_count, slot_count, parts, per_part, highest = dims
+    channels = 3 * levels
     blocks = lon_count // lane_count
     sources = parts * group_count
     half_rows = 2 * per_part
     level_rows = 3 * blocks
     chunks = levels // piece_rows
     chunk_rows = piece_rows * level_rows
-    padded = (level_rows + level_rows % 2) * piece_rows
     for source in range(sources):
         wave_ref[source * piece_rows : (source + 1) * piece_rows, :] = received_ref[source].astype(
             jnp.float32
@@ -483,40 +492,32 @@
         ).T
         for phase in range(2)
     )
+    real, imag = real[:channels], imag[:channels]
+    tiles = near_ref.shape[0] // lane_count
+    for block in range(blocks // tiles):
+        far_real = far_ref[block : block + 1, :lane_count]
+        far_imag = far_ref[block : block + 1, lane_count:]
+        rotated_ref[block * channels : (block + 1) * channels, :] = jnp.concatenate(
+            [real * far_real + imag * far_imag, imag * far_real - real * far_imag], axis=1
+        ).astype(jnp.bfloat16)
+    result = lax.dot_general(
+        rotated_ref[...],
+        near_ref[...],
+        (((1,), (1,)), ((), ())),
+        preferred_element_type=jnp.float32,
+    )
     points = points_ref[0]
-    lane = lax.broadcasted_iota(jnp.int32, (piece_rows, lane_count), 1)
+    lane_wide = lax.broadcasted_iota(jnp.int32, (levels, lane_count), 1)
+    for block in range(blocks):
+        inside = lane_wide < points - block * lane_count
+        lanes = slice(block % tiles * lane_count, (block % tiles + 1) * lane_count)
+        for field in range(3):
+            at = block // tiles * channels + field * levels
+            out_ref[pl.ds(field * blocks + block, levels, stride=level_rows), :] = jnp.where(
+                inside, result[at : at + levels, lanes], 0.0
+            )
     copies = []
     for chunk in range(chunks):
-        units = []
-        for field in range(3):
-            at = field * levels + chunk * piece_rows
-            part_real, part_imag = real[at : at + piece_rows], imag[at : at + piece_rows]
-            for block in range(blocks):
-                far_real = far_ref[block : block + 1, :lane_count]
-                far_imag = far_ref[block : block + 1, lane_count:]
-                units.append(
-                    jnp.concatenate(
-                        [
-                            part_real * far_real + part_imag * far_imag,
-                            part_imag * far_real - part_real * far_imag,
-                        ],
-                        axis=1,
-                    )
-                )
-        for at, two in enumerate(pair_rows(units)):
-            start = chunk * padded + at * 2 * piece_rows
-            rotated_ref[start : start + 2 * piece_rows, :] = two.astype(jnp.bfloat16)
-        result = lax.dot_general(
-            rotated_ref[chunk * padded : (chunk + 1) * padded, :],
-            near_ref[...],
-            (((1,), (1,)), ((), ())),
-            preferred_element_type=jnp.float32,
-        )
-        for unit in range(level_rows):
-            inside = lane < points - unit % blocks * lane_count
-            out_ref[pl.ds(chunk * chunk_rows + unit, piece_rows, stride=level_rows), :] = (
-                jnp.where(inside, result[unit * piece_rows : (unit + 1) * piece_rows], 0.0)
-            )
         rows = pl.ds(chunk * chunk_rows, chunk_rows)
         copies.append(pltpu.make_async_copy(out_ref.at[rows], out_hbm.at[rows], sems.at[chunk]))
         copies[-1].start()
@@ -539,9 +540,12 @@
     channels = 3 * levels
     blocks = lon_count // lane_count
     sources = parts * group_count
-    far_rows = -(-blocks // piece_rows) * piece_rows
+    tiles = max(count for count in (1, 2, 3) if blocks % count == 0)
+    span = tiles * lane_count
+    far_rows = -(-(blocks // tiles) // piece_rows) * piece_rows
     chunks = levels // piece_rows
-    padded = (3 * blocks + 3 * blocks % 2) * piece_rows * chunks
+    slot_rows = -(-(highest + 1) // 16) * 16
+    steps = pltpu.VMEM((span // piece_rows, 2 * lane_count), jnp.float32)
     in_vmem = pl.BlockSpec(memory_space=pltpu.VMEM)
     in_smem = pl.BlockSpec(memory_space=pltpu.SMEM)
     in_hbm = pl.BlockSpec(memory_space=pltpu.HBM)
@@ -560,9 +564,10 @@
             pltpu.VMEM(grid.shape, jnp.float32),
             pltpu.VMEM(owner_pairs.shape, jnp.int32),
             pltpu.VMEM(basis.shape, jnp.bfloat16),
-            pltpu.VMEM((lane_count, 2 * lane_count), jnp.bfloat16),
+            pltpu.VMEM((span, 2 * lane_count), jnp.bfloat16),
             pltpu.VMEM((far_rows, 2 * lane_count), jnp.float32),
-            pltpu.VMEM((padded, lane_count), jnp.bfloat16),
+            steps,
+            pltpu.VMEM((blocks // tiles * channels, span), jnp.bfloat16),
             pltpu.VMEM((sources * piece_rows, lane_count), jnp.float32),
             pltpu.SemaphoreType.DMA((2 + chunks,)),
         ],
@@ -573,13 +578,14 @@
         functools.partial(prepare_kernel, dims),
         name="prepare",
         out_shape=(
-            jax.ShapeDtypeStruct((lane_count, 2 * lane_count), jnp.bfloat16),
+            jax.ShapeDtypeStruct((span, 2 * lane_count), jnp.bfloat16),
             jax.ShapeDtypeStruct((far_rows, 2 * lane_count), jnp.float32),
-            jax.ShapeDtypeStruct((3 * per_part, lane_count, lane_count), jnp.float32),
+            jax.ShapeDtypeStruct((3 * per_part, slot_rows, lane_count), jnp.float32),
             jax.ShapeDtypeStruct((piece_rows, lane_count), jnp.float32),
         ),
         in_specs=[in_smem, in_smem, in_smem, in_vmem, in_smem, in_smem, in_smem],
         out_specs=(in_vmem,) * 4,
+        scratch_shapes=[steps],
         compiler_params=params,
         cost_estimate=pl.CostEstimate(
             flops=40 * lane_count * lane_count, bytes_accessed=1 << 19, transcendentals=0
@@ -603,7 +609,7 @@
         out_specs=in_hbm,
         scratch_shapes=[
             pltpu.VMEM((sources * piece_rows, lane_count), jnp.float32),
-            pltpu.VMEM((padded, 2 * lane_count), jnp.bfloat16),
+            pltpu.VMEM((blocks // tiles * channels, 2 * lane_count), jnp.bfloat16),
             pltpu.VMEM((channels * blocks, lane_count), jnp.float32),
             pltpu.SemaphoreType.DMA((chunks,)),
         ],

time: 31.4 us -> 31.1 us (level)
  no operation moved by 1% of the time
where the time goes in v6:
time: 31.1 us; the launch traced here: 30.8 us
  blocking collectives  9.44 us (30%)
  starting transfers between devices  7.33 us (24%)
  waiting for transfers between devices  6.23 us (20%)
  Pallas kernels  5.16 us (17%)
  between operations  2 us (6%)
  local copies, waits for them, and re-layouts  0.67 us (2%)
    all_to_all x1, blocking collectives, packed_body(): lax.all_to_all(solved, ('lat', 'lev'), split_axis=0, concat_axis=0, tiled...  9.44 us
    all_to_all x1, starting transfers between devices, packed_body(): lax.all_to_all(sent, ('lat', 'lev'), split_axis=0, concat_axis=0, tiled=T...  7.33 us
    all_to_all x1, waiting for transfers between devices, packed_body(): lax.all_to_all(sent, ('lat', 'lev'), split_axis=0, concat_axis=0, tiled=T...  6.23 us
    pallas_call x1, Pallas kernels, packed_body(): pl.pallas_call(functools.partial(analysis_kernel, dims), name='analysis',...  2.24 us
    pallas_call x1, Pallas kernels, packed_body(): pl.pallas_call(functools.partial(synthesis_kernel, dims), name='synthesis...  1.11 us
    pallas_call x1, Pallas kernels, packed_body(): pl.pallas_call(functools.partial(spectral_kernel, dims), name='spectral',...  0.94 us
    pallas_call x1, Pallas kernels, packed_body(): pl.pallas_call(functools.partial(prepare_kernel, dims), name='prepare', o...  0.87 us
    unnamed x6, local copies, waits for them, and re-layouts  0.67 us
  transfers between devices with their start and end apart: 1, of which 1 were waited for; matrix products, arithmetic and copies ran while one was open for 0% of the time, Pallas kernels for 3%

profile of v6, /device:TPU:0, one launch (start us, length us, event | category | flops | bytes accessed | tf_op | source)
XLA Modules:
  0.0 30.8 jit_solution(16254009061669124489)
XLA Ops:
  1.9 2.2 %analysis.1 = bf16[32,16,128]{2,1,0:T(8,128)(2,1)} custom-call(f32[1008,128]{1,0:T(8,128)} %bitcast.5, f32[1]{0:T(128)S(6)} %copy.11.coriolis_ref, f32[1]{0:T(128)S(6)} %copy.12.weights_ref, s32[1]{0:T(128)S(6)} %copy.13.points_ref, s32[8,6]{1,0:T(8,128)} %pairs_ref.1, bf16[1,6,8,97]{3,2,1,0:T(8,128)(2,1)} %bitcast.6), custom_call_target="tpu_custom_call" | custom-call | tf_op jit(solution)/shard_map/analysis/pallas_call | solution.py:557
  4.2 7.3 %all-to-all-start = ((bf16[32,16,128]{2,1,0:T(8,128)(2,1)}), bf16[32,16,128]{2,1,0:T(8,128)(2,1)S(1)}, u32[]{:S(2)}, u32[]{:S(2)}) async-start(bf16[32,16,128]{2,1,0:T(8,128)(2,1)} %analysis.1), calls=%async_computation | async-start | bytes 262144 | tf_op jit(solution)/shard_map/all_to_all | solution.py:576
  11.5 0.0 copy-start
  11.5 0.0 copy-start.1
  11.6 0.0 copy-start.2
  11.6 0.7 %copy-done = s32[8,6]{1,0:T(8,128)S(1)} copy-done((s32[8,6]{1,0:T(8,128)S(1)}, s32[8,6]{1,0:T(8,128)}, u32[]{:S(2)}) %copy-start) | copy-done | bytes 216
  12.2 0.0 copy-done.1
  12.2 0.0 copy-done.2
  12.2 0.9 %prepare.1 = (bf16[384,256]{1,0:T(8,128)(2,1)S(1)}, f32[8,256]{1,0:T(8,128)S(1)}, f32[6,112,128]{2,1,0:T(8,128)S(1)}, f32[8,128]{1,0:T(8,128)S(1)}) custom-call(s32[1]{0:T(128)} %bitcast.3.part_ref, s32[1]{0:T(128)} %bitcast.2.group_ref, s32[1]{0:T(128)S(6)} %copy.13.points_ref, s32[8,6]{1,0:T(8,128)S(1)} %copy-done, s32[8,6]{1,0:T(8,128)S(1)} %copy-done, ...), custom_call_target="tpu_custom_call" | custom-call | flops 655360 | bytes 524288 | tf_op jit(solution)/shard_map/prepare/pallas_call | solution.py:577
  13.1 6.2 %all-to-all-done.received_ref = bf16[32,16,128]{2,1,0:T(8,128)(2,1)S(1)} async-done(((bf16[32,16,128]{2,1,0:T(8,128)(2,1)}), bf16[32,16,128]{2,1,0:T(8,128)(2,1)S(1)}, u32[]{:S(2)}, u32[]{:S(2)}) %all-to-all-start) | async-done | bytes 131104 | tf_op jit(solution)/shard_map/all_to_all | solution.py:576
  19.3 0.9 %spectral.1 = bf16[32,8,128]{2,1,0:T(8,128)(2,1)S(1)} custom-call(bf16[32,16,128]{2,1,0:T(8,128)(2,1)S(1)} %all-to-all-done.received_ref, s32[1]{0:T(128)} %bitcast.2.group_ref, f32[6,112,128]{2,1,0:T(8,128)S(1)} %get-tuple-element.9.solve_ref, f32[8,128]{1,0:T(8,128)S(1)} %get-tuple-element.10.rows_ref), custom_call_target="tpu_custom_call" | custom-call | tf_op jit(solution)/shard_map/spectral/pallas_call | solution.py:594
  20.3 9.4 %all_to_all.10.received_ref = bf16[32,8,128]{2,1,0:T(8,128)(2,1)S(1)} all-to-all(bf16[32,8,128]{2,1,0:T(8,128)(2,1)S(1)} %spectral.1), channel_id=1, replica_groups=mesh['lat'=4,'lev'=8] {'lat','lev'}, dimensions={0} | all-to-all | bytes 131072 | tf_op jit(solution)/shard_map/all_to_all | solution.py:603
  29.7 1.1 %synthesis.1 = f32[1008,128]{1,0:T(8,128)} custom-call(bf16[32,8,128]{2,1,0:T(8,128)(2,1)S(1)} %all_to_all.10.received_ref, bf16[384,256]{1,0:T(8,128)(2,1)S(1)} %get-tuple-element.11.near_ref, f32[8,256]{1,0:T(8,128)S(1)} %get-tuple-element.12.far_ref, s32[1]{0:T(128)S(6)} %copy.13.points_ref), custom_call_target="tpu_custom_call" | custom-call | tf_op jit(solution)/shard_map/synthesis/pallas_call | solution.py:604
Async XLA Ops:
  4.2 15.1 %all-to-all-start = ((bf16[32,16,128]{2,1,0:T(8,128)(2,1)}), bf16[32,16,128]{2,1,0:T(8,128)(2,1)S(1)}, u32[]{:S(2)}, u32[]{:S(2)}) async-start(bf16[32,16,128]{2,1,0:T(8,128)(2,1)} %analysis.1), calls=%async_computation | async-start | bytes 262144 | tf_op jit(solution)/shard_map/all_to_all | solution.py:576
  11.5 0.7 %copy-start = (s32[8,6]{1,0:T(8,128)S(1)}, s32[8,6]{1,0:T(8,128)}, u32[]{:S(2)}) copy-start(s32[8,6]{1,0:T(8,128)} %pairs_ref.1) | copy-start | bytes 580
  11.5 0.7 %copy-start.1 = (f32[16]{0:T(128)S(1)}, f32[16]{0:T(128)}, u32[]{:S(2)}) copy-start(f32[16]{0:T(128)} %depths_ref.1) | copy-start | bytes 196
  11.6 0.7 %copy-start.2 = (f32[16]{0:T(128)S(1)}, f32[16]{0:T(128)}, u32[]{:S(2)}) copy-start(f32[16]{0:T(128)} %diffusion_ref.1) | copy-start | bytes 196

commit v7 on v6

--- a/solution.py
+++ b/solution.py
@@ -222,20 +222,59 @@
     far_ref[:, lane_count:] = far_imag
 
 
+def fill_solve(dims, part, group, pairs, depths, diffusion, solve_ref, rows_ref):
+    levels, lon_count, group_count, slot_count, parts, per_part, highest = dims
+    lane_row = lax.broadcasted_iota(jnp.int32, (1, lane_count), 1)
+    wide = jnp.pad(depths, ((0, 0), (0, lane_count - levels)))
+    is_first = lane_row < levels
+    depth_row = pltpu.roll(wide, levels, 1) + pltpu.roll(wide, 2 * levels, 1)
+    coeff_row = depth_row + jnp.pad(diffusion, ((0, 0), (0, lane_count - levels)))
+    rows_ref[0:1, :] = depth_row
+    row = lax.broadcasted_iota(jnp.int32, pairs.shape, 0)
+    column = lax.broadcasted_iota(jnp.int32, pairs.shape, 1)
+    position = lax.broadcasted_iota(jnp.int32, (solve_ref.shape[1], lane_count), 0).astype(
+        jnp.float32
+    )
+    for index in range(per_part):
+        slot = jnp.minimum(part * per_part + index, slot_count - 1)
+        chosen = jnp.logical_and(row == group, column == slot)
+        pair = jnp.sum(jnp.where(chosen, pairs.astype(jnp.float32), 0.0), axis=0, keepdims=True)
+        pair = jnp.broadcast_to(jnp.sum(pair, axis=1, keepdims=True), (1, lane_count))
+        lower_half = position < float(highest) - pair
+        total = jnp.where(lower_half, pair + position, position - 1.0)
+        operator = total * (total + 1.0) / float(highest * highest)
+        factor = jnp.where(is_first, operator * operator, operator)
+        solve_ref[3 * index] = 1.0 / (1.0 + coeff_row * factor)
+        solve_ref[3 * index + 1] = jnp.where(is_first, 0.0, operator)
+        solve_ref[3 * index + 2] = jnp.where(lower_half, 1.0, 0.0)
+        for half in range(2):
+            wavenumber = pair if half == 0 else float(highest - 1) - pair
+            at = 1 + half * per_part + index
+            rows_ref[at : at + 1, :] = jnp.where(wavenumber == 0.0, 1.0, 2.0)
+
+
 def analysis_kernel(
     dims,
     grid_hbm,
     coriolis_ref,
     weights_ref,
     points_ref,
+    part_ref,
+    group_ref,
     pairs_hbm,
     legendre_hbm,
+    depths_hbm,
+    diffusion_hbm,
     sent_ref,
+    near_ref,
+    far_ref,
+    solve_ref,
+    rows_ref,
     grid_ref,
     pairs_ref,
     legendre_ref,
-    near_ref,
-    far_ref,
+    depths_ref,
+    diffusion_ref,
     step_ref,
     rhs_ref,
     wave_ref,
@@ -250,13 +289,20 @@
     chunks = levels // piece_rows
     chunk_rows = piece_rows * level_rows
     copies = [pltpu.make_async_copy(pairs_hbm, pairs_ref, sems.at[0])]
+    small = (
+        pltpu.make_async_copy(depths_hbm, depths_ref, sems.at[2 + chunks]),
+        pltpu.make_async_copy(diffusion_hbm, diffusion_ref, sems.at[3 + chunks]),
+    )
     for chunk in range(chunks):
         rows = pl.ds(chunk * chunk_rows, chunk_rows)
         copies.append(
             pltpu.make_async_copy(grid_hbm.at[rows], grid_ref.at[rows], sems.at[1 + chunk])
         )
     copies.append(pltpu.make_async_copy(legendre_hbm, legendre_ref, sems.at[1 + chunks]))
-    for copy in copies:
+    copies[0].start()
+    for copy in small:
+        copy.start()
+    for copy in copies[1:]:
         copy.start()
     copies[0].wait()
 
@@ -264,6 +310,18 @@
     points_row = jnp.full((1, lane_count), points, jnp.int32).astype(jnp.float32)
     wave = wave_row(dims, pairs_ref[...])
     fill_factors(wave, points_row, near_ref, far_ref, step_ref)
+    for copy in small:
+        copy.wait()
+    fill_solve(
+        dims,
+        part_ref[0],
+        group_ref[0],
+        pairs_ref[...],
+        depths_ref[...],
+        diffusion_ref[...],
+        solve_ref,
+        rows_ref,
+    )
     tiles = near_ref.shape[0] // lane_count
     rotation = coriolis_ref[0]
     half_rotation = stepsize_delta * rotation
@@ -335,54 +393,6 @@
             sent_ref[at] = jnp.concatenate([upper, lower], axis=0).astype(jnp.bfloat16)
     for at in range(active * group_count, sources):
         sent_ref[at] = jnp.zeros((2 * piece_rows, lane_count), jnp.bfloat16)
-
-
-def prepare_kernel(
-    dims,
-    part_ref,
-    group_ref,
-    points_ref,
-    table_ref,
-    pairs_ref,
-    depths_ref,
-    diffusion_ref,
-    near_ref,
-    far_ref,
-    solve_ref,
-    rows_ref,
-    step_ref,
-):
-    levels, lon_count, group_count, slot_count, parts, per_part, highest = dims
-    points_row = jnp.full((1, lane_count), points_ref[0], jnp.int32).astype(jnp.float32)
-    wave = wave_row(dims, table_ref[...])
-    fill_factors(wave, points_row, near_ref, far_ref, step_ref)
-
-    part, group = part_ref[0], group_ref[0]
-    lane_row = lax.broadcasted_iota(jnp.int32, (1, lane_count), 1)
-    depth_row = jnp.zeros((1, lane_count), jnp.float32)
-    damp_row = jnp.zeros((1, lane_count), jnp.float32)
-    for level in range(levels):
-        depth_row = jnp.where(lane_row % levels == level, depths_ref[level], depth_row)
-        damp_row = jnp.where(lane_row == level, diffusion_ref[level], damp_row)
-    is_first = lane_row < levels
-    coeff_row = jnp.where(is_first, damp_row, depth_row)
-    rows_ref[0:1, :] = depth_row
-    position = lax.broadcasted_iota(jnp.int32, (solve_ref.shape[1], lane_count), 0)
-    for index in range(per_part):
-        pair = pairs_ref[group, jnp.minimum(part * per_part + index, slot_count - 1)]
-        lower_half = position < highest - pair
-        total = jnp.where(lower_half, pair + position, position - 1).astype(jnp.float32)
-        operator = total * (total + 1.0) / float(highest * highest)
-        factor = jnp.where(is_first, operator * operator, operator)
-        solve_ref[3 * index] = 1.0 / (1.0 + coeff_row * factor)
-        solve_ref[3 * index + 1] = jnp.where(is_first, 0.0, operator)
-        solve_ref[3 * index + 2] = jnp.where(lower_half, 1.0, 0.0)
-        for half in range(2):
-            wavenumber = pair if half == 0 else highest - 1 - pair
-            at = 1 + half * per_part + index
-            rows_ref[at : at + 1, :] = jnp.full(
-                (1, lane_count), jnp.where(wavenumber == 0, 1.0, 2.0), jnp.float32
-            )
 
 
 def spectral_kernel(dims, received_ref, group_ref, solve_ref, rows_ref, sent_ref, wave_ref):
@@ -554,43 +564,43 @@
     basis = jnp.swapaxes(legendre, 2, 3)
     part = lax.axis_index("lat").astype(jnp.int32).reshape(1)
     group = lax.axis_index("lev").astype(jnp.int32).reshape(1)
-    sent = pl.pallas_call(
+    sent, near, far, solve, rows = pl.pallas_call(
         functools.partial(analysis_kernel, dims),
         name="analysis",
-        out_shape=jax.ShapeDtypeStruct((sources, 2 * piece_rows, lane_count), jnp.bfloat16),
-        in_specs=[in_hbm, in_smem, in_smem, in_smem, in_hbm, in_hbm],
-        out_specs=in_vmem,
+        out_shape=(
+            pltpu.VMEM((sources, 2 * piece_rows, lane_count), jnp.bfloat16),
+            pltpu.VMEM((span, 2 * lane_count), jnp.bfloat16),
+            pltpu.VMEM((far_rows, 2 * lane_count), jnp.float32),
+            pltpu.VMEM((3 * per_part, slot_rows, lane_count), jnp.float32),
+            pltpu.VMEM((piece_rows, lane_count), jnp.float32),
+        ),
+        in_specs=[in_hbm] + [in_smem] * 5 + [in_hbm] * 4,
+        out_specs=(in_vmem,) * 5,
         scratch_shapes=[
             pltpu.VMEM(grid.shape, jnp.float32),
             pltpu.VMEM(owner_pairs.shape, jnp.int32),
             pltpu.VMEM(basis.shape, jnp.bfloat16),
-            pltpu.VMEM((span, 2 * lane_count), jnp.bfloat16),
-            pltpu.VMEM((far_rows, 2 * lane_count), jnp.float32),
+            pltpu.VMEM((1, levels), jnp.float32),
+            pltpu.VMEM((1, levels), jnp.float32),
             steps,
             pltpu.VMEM((blocks // tiles * channels, span), jnp.bfloat16),
             pltpu.VMEM((sources * piece_rows, lane_count), jnp.float32),
-            pltpu.SemaphoreType.DMA((2 + chunks,)),
+            pltpu.SemaphoreType.DMA((4 + chunks,)),
         ],
-        compiler_params=pltpu.CompilerParams(vmem_limit_bytes=67043328),
-    )(grid, coriolis, weights, row_points, owner_pairs, basis)
+        compiler_params=pltpu.CompilerParams(vmem_limit_bytes=67043328 - (2000 << 10)),
+    )(
+        grid,
+        coriolis,
+        weights,
+        row_points,
+        part,
+        group,
+        owner_pairs,
+        basis,
+        depths.reshape(1, levels),
+        diffusion.reshape(1, levels),
+    )
     received = lax.all_to_all(sent, ("lat", "lev"), split_axis=0, concat_axis=0, tiled=True)
-    near, far, solve, rows = pl.pallas_call(
-        functools.partial(prepare_kernel, dims),
-        name="prepare",
-        out_shape=(
-            jax.ShapeDtypeStruct((span, 2 * lane_count), jnp.bfloat16),
-            jax.ShapeDtypeStruct((far_rows, 2 * lane_count), jnp.float32),
-            jax.ShapeDtypeStruct((3 * per_part, slot_rows, lane_count), jnp.float32),
-            jax.ShapeDtypeStruct((piece_rows, lane_count), jnp.float32),
-        ),
-        in_specs=[in_smem, in_smem, in_smem, in_vmem, in_smem, in_smem, in_smem],
-        out_specs=(in_vmem,) * 4,
-        scratch_shapes=[steps],
-        compiler_params=params,
-        cost_estimate=pl.CostEstimate(
-            flops=40 * lane_count * lane_count, bytes_accessed=1 << 19, transcendentals=0
-        ),
-    )(part, group, row_points, owner_pairs, owner_pairs, depths, diffusion)
     solved = pl.pallas_call(
         functools.partial(spectral_kernel, dims),
         name="spectral",

time: 31.1 us -> 30.2 us (0.971)
  blocking collectives: 9.44 us -> 24.4 us
  starting transfers between devices: 7.33 us -> 0 us
  waiting for transfers between devices: 6.23 us -> 0 us
  Pallas kernels: 5.16 us -> 3.68 us
  local copies, waits for them, and re-layouts: 0.67 us -> 0 us
    all_to_all x0 -> x1, blocking collectives: none -> 14.9 us  [packed_body(): lax.all_to_all(sent, ('lat', 'lev'), split_axis=0, concat_axis=0, tiled=T...]
    all_to_all x1 -> x0, starting transfers between devices: 7.33 us -> none  [packed_body(): lax.all_to_all(sent, ('lat', 'lev'), split_axis=0, concat_axis=0, tiled=T...]
    all_to_all x1 -> x0, waiting for transfers between devices: 6.23 us -> none  [packed_body(): lax.all_to_all(sent, ('lat', 'lev'), split_axis=0, concat_axis=0, tiled=T...]
    pallas_call x1 -> x0, Pallas kernels: 0.87 us -> none  [packed_body(): pl.pallas_call(functools.partial(prepare_kernel, dims), name='prepare', o...]
    unnamed x6 -> x0, local copies, waits for them, and re-layouts: 0.67 us -> none
    pallas_call x1, Pallas kernels: 2.24 us -> 1.63 us  [packed_body(): pl.pallas_call(functools.partial(analysis_kernel, dims), name='analysis',...]
  transfers between devices with their start and end apart: 1 -> 0, of which waited for: 1 -> 0; matrix products, arithmetic and copies ran while one was open for 0% -> 0% of each run, Pallas kernels for 3% -> 0%
where the time goes in v7:
time: 30.2 us; the launch traced here: 30 us
  blocking collectives  24.4 us (81%)
  Pallas kernels  3.68 us (12%)
  between operations  1.96 us (6%)
    all_to_all x1, blocking collectives, packed_body(): lax.all_to_all(sent, ('lat', 'lev'), split_axis=0, concat_axis=0, tiled=T...  14.9 us
    all_to_all x1, blocking collectives, packed_body(): lax.all_to_all(solved, ('lat', 'lev'), split_axis=0, concat_axis=0, tiled...  9.44 us
    pallas_call x1, Pallas kernels, packed_body(): pl.pallas_call(functools.partial(analysis_kernel, dims), name='analysis',...  1.63 us
    pallas_call x1, Pallas kernels, packed_body(): pl.pallas_call(functools.partial(synthesis_kernel, dims), name='synthesis...  1.11 us
    pallas_call x1, Pallas kernels, packed_body(): pl.pallas_call(functools.partial(spectral_kernel, dims), name='spectral',...  0.94 us

profile of v7, /device:TPU:0, one launch (start us, length us, event | category | flops | bytes accessed | tf_op | source)
XLA Modules:
  0.0 30.0 jit_solution(11651076155055700637)
XLA Ops:
  1.9 1.6 %analysis.1 = (bf16[32,16,128]{2,1,0:T(8,128)(2,1)S(1)}, bf16[384,256]{1,0:T(8,128)(2,1)S(1)}, f32[8,256]{1,0:T(8,128)S(1)}, f32[6,112,128]{2,1,0:T(8,128)S(1)}, f32[8,128]{1,0:T(8,128)S(1)}) custom-call(f32[1008,128]{1,0:T(8,128)} %bitcast.7, f32[1]{0:T(128)S(6)} %copy.11.coriolis_ref, f32[1]{0:T(128)S(6)} %copy.12.weights_ref, s32[1]{0:T(128)S(6)} %copy.13.points_ref, ...), custom_call_target="tpu_custom_call" | custom-call | tf_op jit(solution)/shard_map/analysis/pallas_call | solution.py:567
  3.6 14.9 %all_to_all.10.received_ref = bf16[32,16,128]{2,1,0:T(8,128)(2,1)S(1)} all-to-all(bf16[32,16,128]{2,1,0:T(8,128)(2,1)S(1)} %get-tuple-element.10), channel_id=1, replica_groups=mesh['lat'=4,'lev'=8] {'lat','lev'}, dimensions={0} | all-to-all | bytes 262144 | tf_op jit(solution)/shard_map/all_to_all | solution.py:603
  18.5 0.9 %spectral.1 = bf16[32,8,128]{2,1,0:T(8,128)(2,1)S(1)} custom-call(bf16[32,16,128]{2,1,0:T(8,128)(2,1)S(1)} %all_to_all.10.received_ref, s32[1]{0:T(128)} %bitcast.2.group_ref, f32[6,112,128]{2,1,0:T(8,128)S(1)} %get-tuple-element.11.solve_ref, f32[8,128]{1,0:T(8,128)S(1)} %get-tuple-element.12.rows_ref), custom_call_target="tpu_custom_call" | custom-call | tf_op jit(solution)/shard_map/spectral/pallas_call | solution.py:604
  19.5 9.4 %all_to_all.11.received_ref = bf16[32,8,128]{2,1,0:T(8,128)(2,1)S(1)} all-to-all(bf16[32,8,128]{2,1,0:T(8,128)(2,1)S(1)} %spectral.1), channel_id=1, replica_groups=mesh['lat'=4,'lev'=8] {'lat','lev'}, dimensions={0} | all-to-all | bytes 131072 | tf_op jit(solution)/shard_map/all_to_all | solution.py:613
  28.9 1.1 %synthesis.1 = f32[1008,128]{1,0:T(8,128)} custom-call(bf16[32,8,128]{2,1,0:T(8,128)(2,1)S(1)} %all_to_all.11.received_ref, bf16[384,256]{1,0:T(8,128)(2,1)S(1)} %get-tuple-element.13.near_ref, f32[8,256]{1,0:T(8,128)S(1)} %get-tuple-element.14.far_ref, s32[1]{0:T(128)S(6)} %copy.13.points_ref), custom_call_target="tpu_custom_call" | custom-call | tf_op jit(solution)/shard_map/synthesis/pallas_call | solution.py:614

commit v8 on v7

--- a/solution.py
+++ b/solution.py
@@ -395,7 +395,9 @@
         sent_ref[at] = jnp.zeros((2 * piece_rows, lane_count), jnp.bfloat16)
 
 
-def spectral_kernel(dims, received_ref, group_ref, solve_ref, rows_ref, sent_ref, wave_ref):
+def spectral_kernel(
+    dims, received_ref, group_ref, solve_ref, rows_ref, sent_ref, wave_ref, back_ref
+):
     levels, lon_count, group_count, slot_count, parts, per_part, highest = dims
     channels = 3 * levels
     slot_total = highest + 1
@@ -420,8 +422,9 @@
     is_last = lane_row >= 2 * levels
     depth_row = rows_ref[0:1, :]
     held = solve_ref.shape[1]
+    basis_rows = [value.astype(jnp.bfloat16)[:, :held] for value in bases]
+    every = []
     for index in range(per_part):
-        basis = bases[index].astype(jnp.bfloat16)[:, :held]
         basis_turned = bases[index].T[:held].astype(jnp.bfloat16)
         specs = []
         for half in range(2):
@@ -435,6 +438,9 @@
                 axis=1,
             ).astype(jnp.bfloat16)
             specs.append(jnp.dot(basis_turned, waves, preferred_element_type=jnp.float32))
+        every.append(specs)
+    for index in range(per_part):
+        specs, basis = every[index], basis_rows[index]
         lower_half = solve_ref[3 * index + 2] > 0.5
         solved = []
         for phase in range(2):
@@ -459,11 +465,11 @@
             doubling = rows_ref[row : row + 1, :]
             for phase in range(2):
                 at = (phase * 2 + half) * per_part + index
-                wave_ref[pl.ds(at, sources, stride=piece_rows), :] = (
+                back_ref[pl.ds(at, sources, stride=piece_rows), :] = (
                     back[:, phase * lane_count : (phase + 1) * lane_count] * doubling
                 )
     for source in range(sources):
-        sent_ref[source] = wave_ref[
+        sent_ref[source] = back_ref[
             source * piece_rows : (source + 1) * piece_rows, :
         ].astype(jnp.bfloat16)
 
@@ -607,7 +613,7 @@
         out_shape=jax.ShapeDtypeStruct((sources, piece_rows, lane_count), jnp.bfloat16),
         in_specs=[in_vmem, in_smem, in_vmem, in_vmem],
         out_specs=in_vmem,
-        scratch_shapes=[pltpu.VMEM((sources * piece_rows, lane_count), jnp.float32)],
+        scratch_shapes=[pltpu.VMEM((sources * piece_rows, lane_count), jnp.float32)] * 2,
         compiler_params=params,
     )(received, group, solve, rows)
     returned = lax.all_to_all(solved, ("lat", "lev"), split_axis=0, concat_axis=0, tiled=True)

time: 30.2 us -> 29.9 us (0.990)
  Pallas kernels: 3.68 us -> 3.36 us
    pallas_call x1, Pallas kernels: 0.94 us -> 0.63 us  [packed_body(): pl.pallas_call(functools.partial(spectral_kernel, dims), name='spectral',...]
where the time goes in v8:
time: 29.9 us; the launch traced here: 29.7 us
  blocking collectives  24.4 us (82%)
  Pallas kernels  3.36 us (11%)
  between operations  1.96 us (7%)
    all_to_all x1, blocking collectives, packed_body(): lax.all_to_all(sent, ('lat', 'lev'), split_axis=0, concat_axis=0, tiled=T...  14.9 us
    all_to_all x1, blocking collectives, packed_body(): lax.all_to_all(solved, ('lat', 'lev'), split_axis=0, concat_axis=0, tiled...  9.44 us
    pallas_call x1, Pallas kernels, packed_body(): pl.pallas_call(functools.partial(analysis_kernel, dims), name='analysis',...  1.63 us
    pallas_call x1, Pallas kernels, packed_body(): pl.pallas_call(functools.partial(synthesis_kernel, dims), name='synthesis...  1.11 us
    pallas_call x1, Pallas kernels, packed_body(): pl.pallas_call(functools.partial(spectral_kernel, dims), name='spectral',...  0.63 us

profile of v8, /device:TPU:0, one launch (start us, length us, event | category | flops | bytes accessed | tf_op | source)
XLA Modules:
  0.0 29.7 jit_solution(16408054442382476063)
XLA Ops:
  1.9 1.6 %analysis.1 = (bf16[32,16,128]{2,1,0:T(8,128)(2,1)S(1)}, bf16[384,256]{1,0:T(8,128)(2,1)S(1)}, f32[8,256]{1,0:T(8,128)S(1)}, f32[6,112,128]{2,1,0:T(8,128)S(1)}, f32[8,128]{1,0:T(8,128)S(1)}) custom-call(f32[1008,128]{1,0:T(8,128)} %bitcast.7, f32[1]{0:T(128)S(6)} %copy.11.coriolis_ref, f32[1]{0:T(128)S(6)} %copy.12.weights_ref, s32[1]{0:T(128)S(6)} %copy.13.points_ref, ...), custom_call_target="tpu_custom_call" | custom-call | tf_op jit(solution)/shard_map/analysis/pallas_call | solution.py:573
  3.6 14.9 %all_to_all.10.received_ref = bf16[32,16,128]{2,1,0:T(8,128)(2,1)S(1)} all-to-all(bf16[32,16,128]{2,1,0:T(8,128)(2,1)S(1)} %get-tuple-element.10), channel_id=1, replica_groups=mesh['lat'=4,'lev'=8] {'lat','lev'}, dimensions={0} | all-to-all | bytes 262144 | tf_op jit(solution)/shard_map/all_to_all | solution.py:609
  18.5 0.6 %spectral.1 = bf16[32,8,128]{2,1,0:T(8,128)(2,1)S(1)} custom-call(bf16[32,16,128]{2,1,0:T(8,128)(2,1)S(1)} %all_to_all.10.received_ref, s32[1]{0:T(128)} %bitcast.2.group_ref, f32[6,112,128]{2,1,0:T(8,128)S(1)} %get-tuple-element.11.solve_ref, f32[8,128]{1,0:T(8,128)S(1)} %get-tuple-element.12.rows_ref), custom_call_target="tpu_custom_call" | custom-call | tf_op jit(solution)/shard_map/spectral/pallas_call | solution.py:610
  19.2 9.4 %all_to_all.11.received_ref = bf16[32,8,128]{2,1,0:T(8,128)(2,1)S(1)} all-to-all(bf16[32,8,128]{2,1,0:T(8,128)(2,1)S(1)} %spectral.1), channel_id=1, replica_groups=mesh['lat'=4,'lev'=8] {'lat','lev'}, dimensions={0} | all-to-all | bytes 131072 | tf_op jit(solution)/shard_map/all_to_all | solution.py:619
  28.6 1.1 %synthesis.1 = f32[1008,128]{1,0:T(8,128)} custom-call(bf16[32,8,128]{2,1,0:T(8,128)(2,1)S(1)} %all_to_all.11.received_ref, bf16[384,256]{1,0:T(8,128)(2,1)S(1)} %get-tuple-element.13.near_ref, f32[8,256]{1,0:T(8,128)S(1)} %get-tuple-element.14.far_ref, s32[1]{0:T(128)S(6)} %copy.13.points_ref), custom_call_target="tpu_custom_call" | custom-call | tf_op jit(solution)/shard_map/synthesis/pallas_call | solution.py:620

commit v9 on v8

--- a/solution.py
+++ b/solution.py
@@ -523,19 +523,19 @@
         preferred_element_type=jnp.float32,
     )
     points = points_ref[0]
-    lane_wide = lax.broadcasted_iota(jnp.int32, (levels, lane_count), 1)
-    for block in range(blocks):
-        inside = lane_wide < points - block * lane_count
-        lanes = slice(block % tiles * lane_count, (block % tiles + 1) * lane_count)
-        for field in range(3):
-            at = block // tiles * channels + field * levels
-            out_ref[pl.ds(field * blocks + block, levels, stride=level_rows), :] = jnp.where(
-                inside, result[at : at + levels, lanes], 0.0
-            )
+    lane = lax.broadcasted_iota(jnp.int32, (piece_rows, lane_count), 1)
     copies = []
     for chunk in range(chunks):
+        for block in range(blocks):
+            inside = lane < points - block * lane_count
+            lanes = slice(block % tiles * lane_count, (block % tiles + 1) * lane_count)
+            for field in range(3):
+                at = block // tiles * channels + field * levels + chunk * piece_rows
+                out_ref[chunk, pl.ds(field * blocks + block, piece_rows, stride=level_rows), :] = jnp.where(
+                    inside, result[at : at + piece_rows, lanes], 0.0
+                )
         rows = pl.ds(chunk * chunk_rows, chunk_rows)
-        copies.append(pltpu.make_async_copy(out_ref.at[rows], out_hbm.at[rows], sems.at[chunk]))
+        copies.append(pltpu.make_async_copy(out_ref.at[chunk], out_hbm.at[rows], sems.at[chunk]))
         copies[-1].start()
     for copy in copies:
         copy.wait()
@@ -626,7 +626,7 @@
         scratch_shapes=[
             pltpu.VMEM((sources * piece_rows, lane_count), jnp.float32),
             pltpu.VMEM((blocks // tiles * channels, 2 * lane_count), jnp.bfloat16),
-            pltpu.VMEM((channels * blocks, lane_count), jnp.float32),
+            pltpu.VMEM((chunks, channels * blocks // chunks, lane_count), jnp.float32),
             pltpu.SemaphoreType.DMA((chunks,)),
         ],
         compiler_params=params,

time: 29.9 us -> 29.9 us (level)
  no operation moved by 1% of the time
where the time goes in v9:
time: 29.9 us; the launch traced here: 29.7 us
  blocking collectives  24.4 us (82%)
  Pallas kernels  3.36 us (11%)
  between operations  1.96 us (7%)
    all_to_all x1, blocking collectives, packed_body(): lax.all_to_all(sent, ('lat', 'lev'), split_axis=0, concat_axis=0, tiled=T...  14.9 us
    all_to_all x1, blocking collectives, packed_body(): lax.all_to_all(solved, ('lat', 'lev'), split_axis=0, concat_axis=0, tiled...  9.44 us
    pallas_call x1, Pallas kernels, packed_body(): pl.pallas_call(functools.partial(analysis_kernel, dims), name='analysis',...  1.63 us
    pallas_call x1, Pallas kernels, packed_body(): pl.pallas_call(functools.partial(synthesis_kernel, dims), name='synthesis...  1.11 us
    pallas_call x1, Pallas kernels, packed_body(): pl.pallas_call(functools.partial(spectral_kernel, dims), name='spectral',...  0.63 us

profile of v9, /device:TPU:0, one launch (start us, length us, event | category | flops | bytes accessed | tf_op | source)
XLA Modules:
  0.0 29.7 jit_solution(15308400093778390901)
XLA Ops:
  1.9 1.6 %analysis.1 = (bf16[32,16,128]{2,1,0:T(8,128)(2,1)S(1)}, bf16[384,256]{1,0:T(8,128)(2,1)S(1)}, f32[8,256]{1,0:T(8,128)S(1)}, f32[6,112,128]{2,1,0:T(8,128)S(1)}, f32[8,128]{1,0:T(8,128)S(1)}) custom-call(f32[1008,128]{1,0:T(8,128)} %bitcast.7, f32[1]{0:T(128)S(6)} %copy.11.coriolis_ref, f32[1]{0:T(128)S(6)} %copy.12.weights_ref, s32[1]{0:T(128)S(6)} %copy.13.points_ref, ...), custom_call_target="tpu_custom_call" | custom-call | tf_op jit(solution)/shard_map/analysis/pallas_call | solution.py:573
  3.6 14.9 %all_to_all.10.received_ref = bf16[32,16,128]{2,1,0:T(8,128)(2,1)S(1)} all-to-all(bf16[32,16,128]{2,1,0:T(8,128)(2,1)S(1)} %get-tuple-element.10), channel_id=1, replica_groups=mesh['lat'=4,'lev'=8] {'lat','lev'}, dimensions={0} | all-to-all | bytes 262144 | tf_op jit(solution)/shard_map/all_to_all | solution.py:609
  18.5 0.6 %spectral.1 = bf16[32,8,128]{2,1,0:T(8,128)(2,1)S(1)} custom-call(bf16[32,16,128]{2,1,0:T(8,128)(2,1)S(1)} %all_to_all.10.received_ref, s32[1]{0:T(128)} %bitcast.2.group_ref, f32[6,112,128]{2,1,0:T(8,128)S(1)} %get-tuple-element.11.solve_ref, f32[8,128]{1,0:T(8,128)S(1)} %get-tuple-element.12.rows_ref), custom_call_target="tpu_custom_call" | custom-call | tf_op jit(solution)/shard_map/spectral/pallas_call | solution.py:610
  19.2 9.4 %all_to_all.11.received_ref = bf16[32,8,128]{2,1,0:T(8,128)(2,1)S(1)} all-to-all(bf16[32,8,128]{2,1,0:T(8,128)(2,1)S(1)} %spectral.1), channel_id=1, replica_groups=mesh['lat'=4,'lev'=8] {'lat','lev'}, dimensions={0} | all-to-all | bytes 131072 | tf_op jit(solution)/shard_map/all_to_all | solution.py:619
  28.6 1.1 %synthesis.1 = f32[1008,128]{1,0:T(8,128)} custom-call(bf16[32,8,128]{2,1,0:T(8,128)(2,1)S(1)} %all_to_all.11.received_ref, bf16[384,256]{1,0:T(8,128)(2,1)S(1)} %get-tuple-element.13.near_ref, f32[8,256]{1,0:T(8,128)S(1)} %get-tuple-element.14.far_ref, s32[1]{0:T(128)S(6)} %copy.13.points_ref), custom_call_target="tpu_custom_call" | custom-call | tf_op jit(solution)/shard_map/synthesis/pallas_call | solution.py:620
